TPU v7x, 256 devices: a whole 4x4x8 slice. The times are simulated.
256 devices in a mesh: design: 8 (over x, core), pts: 32 (over z, y).
Axes of the slice: x: 4, y: 4, z: 8, core: 2. Of those that a mesh axis runs over, the one named last changes fastest.
Arguments:
- points: bfloat16 [65536, 256], P(('design', 'pts')), parts along dimension 0, may hold values from -6 to 6
- geometry: bfloat16 [131072, 256], P(('design', 'pts')), parts along dimension 0, may hold values from -6 to 6
- counts: int32 [256], P(('design', 'pts')), parts along dimension 0, may hold values from 128 to 256, as said below
- cotangent: bfloat16 [65536, 256], P(('design', 'pts')), parts along dimension 0, may hold values from -0.0625 to 0.0625
- gain_attn: float32 [256], replicated, may hold values from 0.5 to 1.5
- w_feat: bfloat16 [256, 256], replicated, may hold values from -0.375 to 0.375
- w_mid: bfloat16 [256, 256], replicated, may hold values from -0.375 to 0.375
- w_slice: bfloat16 [32, 256], replicated, may hold values from -1 to 1
- sharpness: float32 [8], replicated, may hold values from 0.5 to 6
- w_query: float32 [32, 32], replicated, may hold values from -0.5 to 0.5
- w_key: float32 [32, 32], replicated, may hold values from -0.5 to 0.5
- w_value: float32 [32, 32], replicated, may hold values from -1 to 1
- w_out: bfloat16 [256, 256], replicated, may hold values from -0.375 to 0.375
- gain_mlp: float32 [256], replicated, may hold values from 0.5 to 1.5
- w_up: bfloat16 [256, 1024], replicated, may hold values from -0.375 to 0.375
- w_down: bfloat16 [1024, 256], replicated, may hold values from -0.1875 to 0.1875
Outputs:
- layer_out: bfloat16 [65536, 256], P(('design', 'pts')), parts along dimension 0
- grad_feat: float32 [2048, 256], P(('design', 'pts')), parts along dimension 0
- grad_mid: float32 [2048, 256], P(('design', 'pts')), parts along dimension 0
- grad_out: float32 [2048, 256], P(('design', 'pts')), parts along dimension 0
- grad_up: float32 [2048, 1024], P(('design', 'pts')), parts along dimension 0
- grad_down: float32 [8192, 256], P(('design', 'pts')), parts along dimension 0
- grad_slice: float32 [256, 256], P('design'), parts along dimension 0
- grad_mix: float32 [24, 32, 32], P('design'), parts along dimension 0
There are 8 independent parts, one for each index of `design`. A program takes and returns all parts, laid end to end along the dimension named above; an argument that names none is the same for every part. Nothing has to cross between parts.
Inputs may be any that keep to these rules, and one draw needn't show every extreme that they name: `counts`: every device of a design holds at least half of its 256 slots live, and some device holds all of them.
All inputs are finite; a program needn't handle non-finite values.
Results may differ from a plain program's by a relative error of at most 0.017.
The roundings to bfloat16 on the way count: a program that leaves them out, or rounds other values in their place, can miss the bound.
Values sent between devices are 32-bit elements; how exact they have to be, the bound alone decides.
A program may use at most 64 MiB of HBM per device.

v0:
```python
import math

import jax
import jax.numpy as jnp
from jax import lax
from jax.sharding import PartitionSpec as P


def layer_norm(inputs, gain):
    inputs = inputs.astype(jnp.float32)
    centre = jnp.mean(inputs, axis=-1, keepdims=True)
    shifted = inputs - centre
    spread = jnp.mean(shifted * shifted, axis=-1, keepdims=True)
    return shifted * lax.rsqrt(spread + 1e-05) * gain


def gelu_tanh(inputs):
    return jax.nn.gelu(inputs, approximate=True)


def project(inputs, gain_attn, w_feat, w_mid):
    normed = layer_norm(inputs, gain_attn).astype(jnp.bfloat16)
    features = jnp.dot(normed, w_feat, preferred_element_type=jnp.float32).astype(jnp.bfloat16)
    middle = jnp.dot(normed, w_mid, preferred_element_type=jnp.float32).astype(jnp.bfloat16)
    return (normed, features, middle)


def slice_shares(middle, w_slice, sharpness):
    count = middle.shape[0]
    heads = sharpness.shape[0]
    logits = jnp.dot(middle.reshape(count * heads, -1), w_slice, preferred_element_type=jnp.float32)
    logits = logits.reshape(count, heads, -1) * sharpness[None, :, None]
    largest = jnp.max(logits, axis=-1, keepdims=True)
    powers = jnp.exp(logits - largest)
    return powers / jnp.sum(powers, axis=-1, keepdims=True)


def slice_scan(middle, features, valid, w_slice, sharpness):
    total = middle.shape[0]
    block = math.gcd(total, 512)
    heads = sharpness.shape[0]
    width = w_slice.shape[0]
    slices = w_slice.shape[1]

    def step(carry, pieces):
        middle_block, feature_block, keep_block = pieces
        shares = slice_shares(middle_block, w_slice, sharpness)
        weights = shares * keep_block[:, None, None]
        weights_low = weights.astype(jnp.bfloat16)
        numerator = jnp.einsum(
            "bhm,bhe->hme",
            weights_low,
            feature_block.reshape(block, heads, width),
            preferred_element_type=jnp.float32,
        )
        return ((carry[0] + numerator, carry[1] + jnp.sum(weights, axis=0)), (shares, weights_low))

    start = (
        jnp.zeros((heads, slices, width), jnp.float32),
        jnp.zeros((heads, slices), jnp.float32),
    )
    sums, kept = lax.scan(
        step,
        start,
        (
            middle.reshape(-1, block, middle.shape[1]),
            features.reshape(-1, block, features.shape[1]),
            valid.reshape(-1, block),
        ),
    )
    return (sums, kept[0].reshape(total, heads, slices), kept[1].reshape(total, heads, slices))


def mix_tokens(numerator, denominator, geo_numerator, geo_denominator, w_query, w_key, w_value):
    highest = lax.Precision.HIGHEST
    field_tokens = numerator / (denominator + 1e-05)[:, :, None]
    geo_tokens = geo_numerator / (geo_denominator + 1e-05)[:, :, None]
    both = jnp.concatenate([field_tokens, geo_tokens], axis=1)
    query = jnp.einsum("hme,ef->hmf", field_tokens, w_query, precision=highest)
    key_rows = jnp.einsum("hke,ef->hkf", both, w_key, precision=highest)
    value_rows = jnp.einsum("hke,ef->hkf", both, w_value, precision=highest)
    scores = jnp.einsum("hmf,hkf->hmk", query, key_rows, precision=highest) / math.sqrt(
        w_query.shape[0]
    )
    largest = jnp.max(scores, axis=-1, keepdims=True)
    powers = jnp.exp(scores - largest)
    attention = powers / jnp.sum(powers, axis=-1, keepdims=True)
    return jnp.einsum("hmk,hkf->hmf", attention, value_rows, precision=highest)


def point_back(
    shares, valid, weights_low, features, grad_att, mixed_low, numer_low, denom_grad, sharpness
):
    count, heads, slices = shares.shape
    grad_weights = (
        jnp.einsum(
            "bhe,hme->bhm",
            features.reshape(count, heads, -1),
            numer_low,
            preferred_element_type=jnp.float32,
        )
        + denom_grad[None]
    )
    if grad_att is not None:
        grad_weights = grad_weights + jnp.einsum(
            "bhe,hme->bhm",
            grad_att.reshape(count, heads, -1),
            mixed_low,
            preferred_element_type=jnp.float32,
        )
    grad_weights = grad_weights * valid[:, None, None]
    inner = jnp.sum(shares * grad_weights, axis=-1, keepdims=True)
    logit_low = (shares * (grad_weights - inner) * sharpness[None, :, None]).astype(jnp.bfloat16)
    grad_features = jnp.einsum(
        "bhm,hme->bhe", weights_low, numer_low, preferred_element_type=jnp.float32
    )
    grad_features = grad_features.reshape(count, -1).astype(jnp.bfloat16)
    return (logit_low, grad_features)


def middle_back(logit_low, middle, w_slice):
    count, heads, slices = logit_low.shape
    flat = logit_low.reshape(count * heads, slices)
    grad_middle = lax.dot_general(
        flat, w_slice, (((1,), (1,)), ((), ())), preferred_element_type=jnp.float32
    )
    grad_middle = grad_middle.reshape(count, -1).astype(jnp.bfloat16)
    slice_term = lax.dot_general(
        middle.reshape(count * heads, -1),
        flat,
        (((0,), (0,)), ((), ())),
        preferred_element_type=jnp.float32,
    )
    return (grad_middle, slice_term)


def outer_rows(left, right):
    return jnp.einsum("rd,rw->dw", left, right, preferred_element_type=jnp.float32)


def on_device(
    points,
    geometry,
    counts,
    cotangent,
    gain_attn,
    w_feat,
    w_mid,
    w_slice,
    sharpness,
    w_query,
    w_key,
    w_value,
    w_out,
    gain_mlp,
    w_up,
    w_down,
):
    point_rows = points.shape[0]
    model_width = points.shape[1]
    heads = sharpness.shape[0]
    width = w_slice.shape[0]
    valid = (jnp.arange(point_rows, dtype=jnp.int32) < counts[0]).astype(jnp.float32)
    geo_valid = jnp.ones((geometry.shape[0],), jnp.float32)
    geo_normed, geo_features, geo_middle = project(geometry, gain_attn, w_feat, w_mid)
    geo_sums, geo_shares, geo_weights_low = slice_scan(
        geo_middle, geo_features, geo_valid, w_slice, sharpness
    )
    normed, features, middle = project(points, gain_attn, w_feat, w_mid)
    field_sums, shares, weights_low = slice_scan(middle, features, valid, w_slice, sharpness)
    numerator, denominator, geo_numerator, geo_denominator = lax.psum(
        (field_sums[0], field_sums[1], geo_sums[0], geo_sums[1]), "pts"
    )
    mixed, token_back = jax.vjp(
        mix_tokens, numerator, denominator, geo_numerator, geo_denominator, w_query, w_key, w_value
    )
    mixed_low = mixed.astype(jnp.bfloat16)
    attended = jnp.einsum(
        "bhm,hme->bhe", weights_low, mixed_low, preferred_element_type=jnp.float32
    )
    attended = attended.reshape(point_rows, -1).astype(jnp.bfloat16)
    residual = points.astype(jnp.float32) + jnp.dot(
        attended, w_out, preferred_element_type=jnp.float32
    )

    def mlp_norm(values_in):
        return layer_norm(values_in, gain_mlp)

    second, norm_back = jax.vjp(mlp_norm, residual)
    second_low = second.astype(jnp.bfloat16)
    upper = jnp.dot(second_low, w_up, preferred_element_type=jnp.float32)
    active, gelu_back = jax.vjp(gelu_tanh, upper)
    hidden = active.astype(jnp.bfloat16)
    layer_out = (residual + jnp.dot(hidden, w_down, preferred_element_type=jnp.float32)).astype(
        jnp.bfloat16
    )
    grad_hidden = lax.dot_general(
        cotangent, w_down, (((1,), (1,)), ((), ())), preferred_element_type=jnp.float32
    )
    grad_upper = gelu_back(grad_hidden)[0].astype(jnp.bfloat16)
    grad_second = lax.dot_general(
        grad_upper, w_up, (((1,), (1,)), ((), ())), preferred_element_type=jnp.float32
    )
    grad_resid = (cotangent.astype(jnp.float32) + norm_back(grad_second)[0]).astype(jnp.bfloat16)
    grad_att = lax.dot_general(
        grad_resid, w_out, (((1,), (1,)), ((), ())), preferred_element_type=jnp.float32
    ).astype(jnp.bfloat16)
    mixed_term = jnp.einsum(
        "bhm,bhe->hme",
        weights_low,
        grad_att.reshape(point_rows, heads, width),
        preferred_element_type=jnp.float32,
    )
    mixed_grad = lax.psum(mixed_term, "pts")
    grads = token_back(mixed_grad)
    numer_low = grads[0].astype(jnp.bfloat16)
    geo_numer_low = grads[2].astype(jnp.bfloat16)
    grad_mix = jnp.stack([grads[4], grads[5], grads[6]])
    logit_low, grad_features = point_back(
        shares, valid, weights_low, features, grad_att, mixed_low, numer_low, grads[1], sharpness
    )
    grad_middle, slice_term = middle_back(logit_low, middle, w_slice)
    geo_logit_low, geo_grad_features = point_back(
        geo_shares,
        geo_valid,
        geo_weights_low,
        geo_features,
        None,
        mixed_low,
        geo_numer_low,
        grads[3],
        sharpness,
    )
    geo_grad_middle, geo_slice_term = middle_back(geo_logit_low, geo_middle, w_slice)
    grad_slice = lax.psum(slice_term + geo_slice_term, "pts")
    field_right = jnp.concatenate([grad_features, grad_middle], axis=1)
    geo_right = jnp.concatenate([geo_grad_features, geo_grad_middle], axis=1)
    grad_down = lax.psum_scatter(
        outer_rows(hidden, cotangent), "pts", scatter_dimension=0, tiled=True
    )
    every_part = lax.psum_scatter(
        jnp.concatenate(
            [
                outer_rows(normed, field_right) + outer_rows(geo_normed, geo_right),
                jnp.concatenate(
                    [outer_rows(attended, grad_resid), outer_rows(second_low, grad_upper)], axis=1
                ),
            ],
            axis=1,
        ),
        "pts",
        scatter_dimension=0,
        tiled=True,
    )
    proj_part = every_part[:, : 2 * model_width]
    grad_out = every_part[:, 2 * model_width : 3 * model_width]
    grad_up = every_part[:, 3 * model_width :]
    grad_feat = proj_part[:, :model_width]
    grad_mid = proj_part[:, model_width:]
    return (layer_out, grad_feat, grad_mid, grad_out, grad_up, grad_down, grad_slice, grad_mix)


def solution(mesh):
    placed = (
        P(("design", "pts"), None),
        P(("design", "pts"), None),
        P(("design", "pts")),
        P(("design", "pts"), None),
        P(),
        P(),
        P(),
        P(),
        P(),
        P(),
        P(),
        P(),
        P(),
        P(),
        P(),
        P(),
    )
    return jax.shard_map(
        on_device,
        mesh=mesh,
        in_specs=placed,
        out_specs=(
            P(("design", "pts"), None),
            P(("design", "pts"), None),
            P(("design", "pts"), None),
            P(("design", "pts"), None),
            P(("design", "pts"), None),
            P(("design", "pts"), None),
            P("design", None),
            P("design", None, None),
        ),
        check_vma=False,
    )
```

profile of v0, /device:TPU:4, one launch (start us, length us, event | category | flops | bytes accessed | tf_op | source)
XLA Modules:
  0.0 863.7 jit_solution(780190361314561102)
XLA Ops:
  8.5 1.2 convolution_convert_fusion.8
  9.7 1.2 convolution_convert_fusion.7
  12.1 1.2 fusion.59
  13.3 1.4 convolution_convert_fusion.4
  14.8 1.5 convolution_convert_fusion.3
  17.0 2.8 fusion.160
  19.7 3.1 fusion.163
  22.9 2.0 multiply_reduce_fusion.2
  25.9 2.5 fusion.49
  28.5 2.7 fusion.125
  31.2 146.6 %all-reduce = (f32[8,256]{1,0:T(8,128)S(1)}, f32[8,256]{1,0:T(8,128)S(1)}) all-reduce(f32[8,256]{1,0:T(8,128)S(1)} %get-tuple-element.98, f32[8,256]{1,0:T(8,128)S(1)} %fusion.125), channel_id=1, replica_groups=mesh['design'=8,'pts'=32] {'pts'}, use_global_device_ids=true, to_apply=%region_6.7 | all-reduce | flops 4096 | bytes 32768 | tf_op jit(solution)/shard_map/psum | solution.py:171
  179.8 1.3 fusion.170
  183.3 1.3 fusion.78
  184.6 1.9 copy.60
  186.5 5.2 fusion.169
  191.7 9.7 %online-softmax = f32[8,256,32]{2,1,0:T(8,128)} custom-call(f32[8,256,512]{2,1,0:T(8,128)} %get-tuple-element.120, f32[8,512,32]{2,1,0:T(8,128)} %copy.60), custom_call_target="tpu_custom_call" | custom-call | tf_op online-softmax
  201.4 1.6 convolution_convert_fusion.9
  203.0 1.2 fusion.168
  204.4 3.3 fusion.44
  209.6 1.2 fusion.14
  213.2 2.4 fusion.115
  215.6 139.5 %all-reduce.5.cloned.1.call-done = f32[8,256,32]{1,2,0:T(8,128)} async-done(((f32[8,256,32]{1,2,0:T(8,128)}), f32[8,256,32]{1,2,0:T(8,128)}) %all-reduce.5.cloned.1.call-update) | async-done | bytes 262160 | tf_op jit(solution)/shard_map/psum | solution.py:214
  355.1 6.6 convert_reduce_fusion
  361.8 1.4 fusion.158
  363.3 3.4 fusion.12
  366.7 4.7 fusion.13
  371.6 3.6 fusion.7
  378.5 11.1 %fusion.20 = bf16[256,8,256]{2,0,1:T(8,128)(2,1)S(1)} fusion(f32[8,256,256]{1,2,0:T(8,128)S(1)} %add_multiply_fusion.4, f32[8]{0:T(128)S(1)} %copy-done.59, f32[256,8,256]{2,0,1:T(8,128)S(1)} %copy-done.9, f32[256,8]{0,1:T(8,128)S(1)} %copy-done.45), kind=kOutput, calls=%fused_computation.32 | output fusion | flops 3672319 | bytes 5251104 | tf_op jit(solution)/shard_map/sub | solution.py:113
  389.7 4.2 convolution_convert_fusion.2
  393.9 10.2 %fusion.6 = bf16[512,8,256]{2,0,1:T(8,128)(2,1)} fusion(f32[8,256]{1,0:T(8,128)S(1)} %neg.34, f32[8]{0:T(128)S(1)} %copy-done.60, bf16[8,256,32]{1,2,0:T(8,128)(2,1)S(1)} %get-tuple-element.100, bf16[512,8,32]{0,2,1:T(8,128)(2,1)} %bitcast.190, f32[512,8,256]{2,0,1:T(8,128)} %get-tuple-element.112, f32[512,8]{0,1:T(8,128)S(1)} %copy-done.40), kind=kOutput, calls=%fused_computation.9 | convolution fusion | flops 143659264 | bytes 6709280 | tf_op jit(solution)/shard_map/sub | solution.py:113
  404.9 1.3 convolution_convert_fusion.1
  406.3 1.2 copy.66
  409.6 3.0 convolution_convert_fusion
  412.6 1.3 copy.70
  413.9 2.3 convert_element_type.154
  416.2 1.5 fusion.62
  417.7 1.2 convolution_add_fusion
  419.0 2.4 pad_maximum_fusion
  421.5 2.8 fusion.121
  426.1 2.0 fusion.34
  428.8 2.1 fusion.45
  430.9 2.9 fusion.35
  433.8 140.6 %psum.47 = f32[32,256]{1,0:T(8,128)} all-reduce(f32[32,256]{1,0:T(8,128)S(1)} %fusion.35), channel_id=1, replica_groups=mesh['design'=8,'pts'=32] {'pts'}, use_global_device_ids=true, to_apply=%region_30.31 | all-reduce | flops 8192 | bytes 65536 | tf_op jit(solution)/shard_map/psum | solution.py:235
  575.3 1.6 convolution_bitcast_fusion
  577.5 59.5 %reduce-scatter.3.cloned.1.call-done = f32[8,1792]{1,0:T(8,128)} async-done(((f32[256,1792]{1,0:T(8,128)}), f32[8,1792]{1,0:T(8,128)}) %reduce-scatter.3.cloned.1.call-update) | async-done | bytes 57360 | tf_op jit(solution)/shard_map/reduce_scatter | solution.py:241
  637.0 1.4 slice.22
  638.4 1.3 fusion.159
  639.7 217.1 %reduce-scatter.5.cloned.1.call-done = f32[32,256]{1,0:T(8,128)} async-done(((f32[1024,256]{1,0:T(8,128)}), f32[32,256]{1,0:T(8,128)}) %reduce-scatter.5.cloned.1.call-update) | async-done | bytes 32784 | tf_op jit(solution)/shard_map/reduce_scatter | solution.py:238
  (183 shorter events, 22.3 us)
Async XLA Ops:
  7.2 197.2 %copy-start = (bf16[256,1024]{1,0:T(8,128)(2,1)S(1)}, bf16[256,1024]{1,0:T(8,128)(2,1)}, u32[]{:S(2)}) copy-start(bf16[256,1024]{1,0:T(8,128)(2,1)} %param.30) | copy-start | bytes 1572868
  7.2 12.5 %copy-start.56 = (bf16[32,256]{1,0:T(8,128)(2,1)S(1)}, bf16[32,256]{1,0:T(8,128)(2,1)}, u32[]{:S(2)}) copy-start(bf16[32,256]{1,0:T(8,128)(2,1)} %param.23) | copy-start | bytes 49156
  7.2 12.5 %copy-start.58 = (f32[8]{0:T(128)S(1)}, f32[8]{0:T(128)}, u32[]{:S(2)}) copy-start(f32[8]{0:T(128)} %param.24) | copy-start | bytes 100
  7.2 173.9 %all-reduce.7.cloned.1.call-start = ((), (), s32[]{:S(2)}) async-start(), calls=%async_computation.5 | async-start | bytes 1048576 | tf_op jit(solution)/shard_map/psum | solution.py:171
  8.4 14.5 %copy-start.42 = (f32[256]{0:T(256)}, f32[256]{0:T(256)S(1)}, u32[]{:S(2)}) copy-start(f32[256]{0:T(256)S(1)} %broadcast_multiply_fusion.2) | copy-start | bytes 3076
  9.7 13.2 %copy-start.25 = (bf16[256,256]{0,1:T(8,128)(2,1)}, bf16[256,256]{0,1:T(8,128)(2,1)S(1)}, u32[]{:S(2)}) copy-start(bf16[256,256]{0,1:T(8,128)(2,1)S(1)} %convolution_convert_fusion.8) | copy-start | bytes 393220
  10.9 14.0 %copy-start.20 = (bf16[256,256]{0,1:T(8,128)(2,1)}, bf16[256,256]{0,1:T(8,128)(2,1)S(1)}, u32[]{:S(2)}) copy-start(bf16[256,256]{0,1:T(8,128)(2,1)S(1)} %convolution_convert_fusion.7) | copy-start | bytes 393220
  12.1 10.8 %copy-start.46 = (f32[512]{0:T(512)}, f32[512]{0:T(512)S(1)}, u32[]{:S(2)}) copy-start(f32[512]{0:T(512)S(1)} %broadcast_multiply_fusion) | copy-start | bytes 6148
  13.3 9.6 %copy-start.53 = (f32[512]{0:T(512)}, f32[512]{0:T(512)S(1)}, u32[]{:S(2)}) copy-start(f32[512]{0:T(512)S(1)} %add_rsqrt_fusion) | copy-start | bytes 6148
  14.7 11.2 %copy-start.23 = (bf16[512,256]{0,1:T(8,128)(2,1)}, bf16[512,256]{0,1:T(8,128)(2,1)S(1)}, u32[]{:S(2)}) copy-start(bf16[512,256]{0,1:T(8,128)(2,1)S(1)} %convolution_convert_fusion.4) | copy-start | bytes 786436
  16.3 9.7 %copy-start.61 = (bf16[512,256]{0,1:T(8,128)(2,1)}, bf16[512,256]{0,1:T(8,128)(2,1)S(1)}, u32[]{:S(2)}) copy-start(bf16[512,256]{0,1:T(8,128)(2,1)S(1)} %convolution_convert_fusion.3) | copy-start | bytes 786436
  16.9 8.0 copy-start.48
  19.7 6.2 copy-start.44
  22.9 5.7 copy-start.39
  28.4 150.0 %copy-start.22 = (bf16[256,256]{1,0:T(8,128)(2,1)S(1)}, bf16[256,256]{1,0:T(8,128)(2,1)}, u32[]{:S(2)}) copy-start(bf16[256,256]{1,0:T(8,128)(2,1)} %param.19) | copy-start | bytes 393220
  28.4 151.4 %copy-start.18 = (bf16[1024,256]{1,0:T(8,128)(2,1)S(1)}, bf16[1024,256]{1,0:T(8,128)(2,1)}, u32[]{:S(2)}) copy-start(bf16[1024,256]{1,0:T(8,128)(2,1)} %param.31) | copy-start | bytes 1572868
  28.4 153.7 %copy-start.34 = (f32[32,32]{1,0:T(8,128)S(1)}, f32[32,32]{1,0:T(8,128)}, u32[]{:S(2)}) copy-start(f32[32,32]{1,0:T(8,128)} %param.25) | copy-start | bytes 12292
  28.4 154.2 %copy-start.32 = (f32[32,32]{1,0:T(8,128)S(1)}, f32[32,32]{1,0:T(8,128)}, u32[]{:S(2)}) copy-start(f32[32,32]{1,0:T(8,128)} %param.26) | copy-start | bytes 12292
  28.5 326.7 %all-reduce.5.cloned.1.call-start = ((), (), s32[]{:S(2)}) async-start(), calls=%async_computation.2 | async-start | bytes 524288 | tf_op jit(solution)/shard_map/psum | solution.py:214
  178.4 6.2 copy-start.27
  182.6 9.1 %copy-start.5 = (f32[8,256,32]{1,2,0:T(8,128)}, f32[8,256,32]{1,2,0:T(8,128)S(1)}, u32[]{:S(2)}) copy-start(f32[8,256,32]{1,2,0:T(8,128)S(1)} %fusion.89) | copy-start | bytes 786436
  203.0 4.6 copy-start.52
  204.4 5.2 copy-start.1
  213.0 424.1 %reduce-scatter.3.cloned.1.call-start = ((), (), s32[]{:S(2)}) async-start(), calls=%async_computation.3 | async-start | bytes 1892352 | tf_op jit(solution)/shard_map/reduce_scatter | solution.py:241
  355.1 6.7 copy-start.2
  355.1 6.7 copy-start.30
  366.7 4.7 copy-start.55
  371.5 5.0 copy-start.7
  371.5 4.3 copy-start.33
  371.5 5.0 copy-start.16
  371.5 5.0 copy-start.35
  371.5 5.0 copy-start.38
  371.5 5.4 copy-start.21
  371.6 5.4 copy-start.28
  378.5 11.1 %copy-start.15 = (f32[8,256,32]{1,2,0:T(8,128)S(1)}, f32[8,256,32]{1,2,0:T(8,128)}, u32[]{:S(2)}) copy-start(f32[8,256,32]{1,2,0:T(8,128)} %get-tuple-element.92) | copy-start | bytes 786436
  378.5 11.1 %copy-start.37 = (f32[8,256]{1,0:T(8,128)S(1)}, f32[8,256]{1,0:T(8,128)}, u32[]{:S(2)}) copy-start(f32[8,256]{1,0:T(8,128)} %get-tuple-element.107) | copy-start | bytes 24580
  389.6 15.3 %copy-start.14 = (bf16[256,8,256]{2,0,1:T(8,128)(2,1)}, bf16[256,8,256]{2,0,1:T(8,128)(2,1)S(1)}, u32[]{:S(2)}) copy-start(bf16[256,8,256]{2,0,1:T(8,128)(2,1)S(1)} %fusion.20) | copy-start | bytes 3145732
  389.7 4.2 copy-start.40
  389.7 4.2 copy-start.60
  393.9 11.0 %copy-start.57 = (bf16[32,256]{1,0:T(8,128)(2,1)S(1)}, bf16[32,256]{1,0:T(8,128)(2,1)}, u32[]{:S(2)}) copy-start(bf16[32,256]{1,0:T(8,128)(2,1)} %param.23) | copy-start | bytes 49156
  404.9 11.2 %copy-start.47 = (f32[512]{0:T(512)S(1)}, f32[512]{0:T(512)}, u32[]{:S(2)}) copy-start(f32[512]{0:T(512)} %copy-done.46) | copy-start | bytes 6148
  404.9 11.2 %copy-start.54 = (f32[512]{0:T(512)S(1)}, f32[512]{0:T(512)}, u32[]{:S(2)}) copy-start(f32[512]{0:T(512)} %copy-done.53) | copy-start | bytes 6148
  407.5 10.3 %copy-start.43 = (f32[256]{0:T(256)S(1)}, f32[256]{0:T(256)}, u32[]{:S(2)}) copy-start(f32[256]{0:T(256)} %copy-done.42) | copy-start | bytes 3076
  407.5 10.3 %copy-start.51 = (f32[256]{0:T(256)S(1)}, f32[256]{0:T(256)}, u32[]{:S(2)}) copy-start(f32[256]{0:T(256)} %copy-done.50) | copy-start | bytes 3076
  409.6 9.4 %copy-start.4 = (f32[256,1024]{1,0:T(8,128)S(1)}, f32[256,1024]{1,0:T(8,128)}, u32[]{:S(2)}) copy-start(f32[256,1024]{1,0:T(8,128)} %fusion.115) | copy-start | bytes 3145732
  419.0 5.3 copy-start.26
  421.4 435.4 %reduce-scatter.5.cloned.1.call-start = ((), (), s32[]{:S(2)}) async-start(), calls=%async_computation.4 | async-start | bytes 1081344 | tf_op jit(solution)/shard_map/reduce_scatter | solution.py:238
  426.1 148.9 %copy-start.8 = (f32[8,256,32]{1,2,0:T(8,128)S(1)}, f32[8,256,32]{1,2,0:T(8,128)}, u32[]{:S(2)}) copy-start(f32[8,256,32]{1,2,0:T(8,128)} %copy-done.7) | copy-start | bytes 786436
  (18 other events, 46.3 us)
Sparse Core Ops, SparseCore 0:
  28.6 151.8 all-reduce.6
  213.1 141.9 all-reduce.4
  421.5 215.4 reduce-scatter.2
  641.3 215.5 reduce-scatter.4
where the time goes:
time: 870 us; the launch traced here: 864 us
  waiting for transfers between devices  416 us (48%)
  blocking collectives  287 us (33%)
  matrix products  89.7 us (10%)
  other arithmetic  27.1 us (3%)
  local copies, waits for them, and re-layouts  17.7 us (2%)
  between operations  15.8 us (2%)
  Pallas kernels  9.67 us (1%)
    reduce_scatter x1, waiting for transfers between devices, on_device(): lax.psum_scatter(outer_rows(hidden, cotangent), 'pts', scatter_dimension=...  217 us
    psum x1, blocking collectives, on_device(): lax.psum((field_sums[0], field_sums[1], geo_sums[0], geo_sums[1]), 'pts')  147 us
    psum x1, blocking collectives, on_device(): grad_slice = lax.psum(slice_term + geo_slice_term, 'pts')  141 us
    psum x1, waiting for transfers between devices, on_device(): mixed_grad = lax.psum(mixed_term, 'pts')  140 us
    reduce_scatter x1, waiting for transfers between devices, on_device(): lax.psum_scatter(jnp.concatenate([outer_rows(normed, field_right) + outer...  59.5 us
  transfers between devices with their start and end apart: 4, of which 3 were waited for; matrix products, arithmetic and copies ran while one was open for 3% of the time, Pallas kernels for 0%

commit v1 on v0

v1 whole, which is shorter than its diff:
```python
import functools
import math

import jax
import jax.numpy as jnp
from jax import lax
from jax.experimental import pallas as pl
from jax.experimental.pallas import tpu as pltpu
from jax.sharding import PartitionSpec as P

F32 = jnp.float32
BF16 = jnp.bfloat16
HIGH = lax.Precision.HIGHEST
NY = 4
NZ = 8
HEADS = 8
DH = 32
M = 256
D = 256
FF = 1024
RB = 256
SUMS = 72
BIG = 72
SMALL = 16
EPS = 1e-05
VMEM_BYTES = 64000000
ORDER = (4, 3, 5, 2, 6, 1, 7)


def nn(a, b, precision=None):
    return lax.dot_general(
        a, b, (((1,), (0,)), ((), ())), precision=precision, preferred_element_type=F32
    )


def nt(a, b, precision=None):
    return lax.dot_general(
        a, b, (((1,), (1,)), ((), ())), precision=precision, preferred_element_type=F32
    )


def tn(a, b, precision=None):
    return lax.dot_general(
        a, b, (((0,), (0,)), ((), ())), precision=precision, preferred_element_type=F32
    )


def norm_parts(x):
    centre = jnp.mean(x, axis=-1, keepdims=True)
    shifted = x - centre
    spread = jnp.mean(shifted * shifted, axis=-1, keepdims=True)
    scale = lax.rsqrt(spread + EPS)
    return shifted * scale, scale


def place():
    me = lax.axis_index("pts")
    return lax.div(me, NY), lax.rem(me, NY)


def peer_z(z, y, k):
    return {"pts": lax.rem(z + k, NZ) * NY + y}


def peer_y(z, y, k):
    return {"pts": z * NY + lax.rem(y + k, NY)}


def greet(z, y):
    barrier = pltpu.get_barrier_semaphore()
    for k in range(1, NZ):
        pl.semaphore_signal(barrier, inc=1, device_id=peer_z(z, y, k), device_id_type=pl.DeviceIdType.MESH)
    for k in range(1, NY):
        pl.semaphore_signal(barrier, inc=1, device_id=peer_y(z, y, k), device_id_type=pl.DeviceIdType.MESH)


def meet():
    pl.semaphore_wait(pltpu.get_barrier_semaphore(), NZ - 1 + NY - 1)


def send(src, dst, sems, slot, device):
    return pltpu.make_async_remote_copy(
        src_ref=src,
        dst_ref=dst,
        send_sem=sems.at[0, slot],
        recv_sem=sems.at[1, slot],
        device_id=device,
        device_id_type=pl.DeviceIdType.MESH,
    )


def first_kernel(
    points,
    geometry,
    counts,
    gain,
    w_feat,
    w_mid,
    w_slice,
    sharp,
    w_query,
    w_key,
    w_value,
    normed_out,
    feat_out,
    mid_out,
    shares_out,
    wlow_out,
    wsm_out,
    mixed_out,
    attn_out,
    both_out,
    query_out,
    keyval_out,
    sums_out,
    part,
    zbuf,
    ybuf,
    mbuf,
    feat_t,
    sem_z,
    sem_y,
    sem_m,
):
    z, y = place()
    greet(z, y)
    wsm_out[...] = jnp.zeros_like(wsm_out)
    for h in range(HEADS):
        wsm_out[h, h * DH : (h + 1) * DH, :] = w_slice[...]
    for b in range(3):
        rows = slice(b * RB, (b + 1) * RB)
        x = points[...] if b == 0 else geometry[(b - 1) * RB : b * RB, :]
        normed = (norm_parts(x.astype(F32))[0] * gain[...]).astype(BF16)
        normed_out[rows, :] = normed
        feats = nn(normed, w_feat[...])
        feat_out[rows, :] = feats.astype(BF16)
        feat_t[:, rows] = feats.T.astype(BF16)
        mid_out[rows, :] = nn(normed, w_mid[...]).astype(BF16)
    live = lax.broadcasted_iota(jnp.int32, (RB, 1), 0) < counts[0]
    valid = jnp.where(live, 1.0, 0.0).astype(F32)
    meet()

    def head_step(k, carry):
        h = lax.rem(z + 1 + k, NZ)
        weight = wsm_out[h]
        factor = sharp[h]
        row = pl.multiple_of(h * DH, DH)
        numers = []
        denoms = []
        for b in range(3):
            rows = slice(b * RB, (b + 1) * RB)
            logits = nn(mid_out[rows, :], weight) * factor
            powers = jnp.exp(logits - jnp.max(logits, axis=-1, keepdims=True))
            shares = powers * (1.0 / jnp.sum(powers, axis=-1, keepdims=True))
            shares_out[h, rows, :] = shares
            weights = shares * valid if b == 0 else shares
            low = weights.astype(BF16)
            wlow_out[h, rows, :] = low
            denoms.append(jnp.sum(weights, axis=0, keepdims=True))
            numers.append(nn(feat_t[pl.ds(row, DH), rows], low))
        part[h, 0:DH, :] = numers[0]
        part[h, DH : 2 * DH, :] = numers[1] + numers[2]
        pick = lax.broadcasted_iota(jnp.int32, (8, M), 0)
        part[h, 2 * DH : SUMS, :] = jnp.where(
            pick == 0, denoms[0], jnp.where(pick == 1, denoms[1] + denoms[2], 0.0)
        )

        @pl.when(k < NZ - 1)
        def _():
            send(part.at[h], zbuf.at[k], sem_z, k, peer_z(z, y, k + 1)).start()

        return carry

    lax.fori_loop(0, NZ, head_step, 0)
    total = part[z]
    for k in range(NZ - 1):
        send(part.at[0], zbuf.at[k], sem_z, k, peer_z(z, y, k + 1)).wait_recv()
        total = total + zbuf[k]
    ybuf[0] = total
    copies = [send(ybuf.at[0], ybuf.at[k], sem_y, k - 1, peer_y(z, y, k)) for k in range(1, NY)]
    for copy in copies:
        copy.start()
    for copy in copies:
        copy.wait_recv()
    sums = ybuf[y]
    for other in range(1, NY):
        sums = sums + ybuf[lax.rem(y + NY - other, NY)]
    sums_out[...] = sums
    field = sums[0:DH] / (sums[2 * DH : 2 * DH + 1] + EPS)
    geo = sums[DH : 2 * DH] / (sums[2 * DH + 1 : 2 * DH + 2] + EPS)
    both_out[:, 0:M] = field
    both_out[:, M : 2 * M] = geo
    both = both_out[...]
    query = tn(w_query[...], field, HIGH)
    keys = tn(w_key[...], both, HIGH)
    values = tn(w_value[...], both, HIGH)
    query_out[...] = query
    keyval_out[0] = keys
    keyval_out[1] = values
    scores = tn(keys, query, HIGH) * (1.0 / math.sqrt(DH))
    powers = jnp.exp(scores - jnp.max(scores, axis=0, keepdims=True))
    attention = powers * (1.0 / jnp.sum(powers, axis=0, keepdims=True))
    attn_out[...] = attention
    mbuf[z] = nn(values, attention, HIGH)
    copies = [
        send(mbuf.at[z], mbuf.at[z], sem_m, k - 1, peer_z(z, y, k)) for k in ORDER
    ]
    for copy in copies:
        copy.start()
    for copy in copies:
        copy.wait_recv()
    mixed_out[...] = mbuf[...]
    for copy in copies:
        copy.wait_send()
    for k in range(1, NY):
        send(ybuf.at[0], ybuf.at[k], sem_y, k - 1, peer_y(z, y, k)).wait_send()
    for k in range(NZ - 1):
        send(part.at[0], zbuf.at[k], sem_z, k, peer_z(z, y, k + 1)).wait_send()


def second_kernel(
    points,
    cotangent,
    counts,
    wlow,
    shares,
    normed,
    feats,
    mids,
    wsm,
    mixed,
    attn,
    both_in,
    query_in,
    keyval,
    sums_in,
    sharp,
    gain,
    w_out,
    w_up,
    w_down,
    w_query,
    w_key,
    w_value,
    layer_out,
    feat_grad,
    mid_grad,
    out_grad,
    up_grad,
    down_grad,
    slice_grad,
    mix_grad,
    mixm,
    num_m,
    geo_m,
    low_up,
    low_hidden,
    grad_up_low,
    norm_hat,
    att_rows,
    res_rows,
    att_grad,
    mid_t,
    normed_t,
    acc_feat,
    acc_mid,
    mg_part,
    mg_z,
    mg_y,
    gbuf,
    mix_buf,
    big,
    big_y,
    big_stage,
    big_z,
    small,
    small_y,
    small_stage,
    small_z,
    slice_part,
    slice_y,
    slice_z,
    slice_all,
    sem_mz,
    sem_my,
    sem_g,
    sem_mix,
    sem_by,
    sem_bz,
    sem_sy,
    sem_sz,
    sem_ly,
    sem_lz,
    sem_la,
):
    z, y = place()
    greet(z, y)
    mixm[...] = jnp.zeros_like(mixm)
    for h in range(HEADS):
        mixm[h, h * DH : (h + 1) * DH, :] = mixed[h].astype(BF16)
    attended = nt(wlow[0, 0:RB, :], mixm[0])
    for h in range(1, HEADS):
        attended = attended + nt(wlow[h, 0:RB, :], mixm[h])
    attended = attended.astype(BF16)
    att_rows[...] = attended
    residual = points[...].astype(F32) + nn(attended, w_out[...])
    hat, scale = norm_parts(residual)
    second_low = (hat * gain[...]).astype(BF16)
    low_up[...] = second_low
    norm_hat[...] = hat
    seed = cotangent[...]
    const = math.sqrt(2.0 / math.pi)
    layer = residual
    grad_second = jnp.zeros((RB, D), F32)
    for j in range(FF // D):
        cols = slice(j * D, (j + 1) * D)
        upper = nn(second_low, w_up[:, cols])
        square = upper * upper
        tanh = jnp.tanh(const * upper * (1.0 + 0.044715 * square))
        half = 0.5 * (1.0 + tanh)
        hidden = (upper * half).astype(BF16)
        low_hidden[:, cols] = hidden
        layer = layer + nn(hidden, w_down[cols, :])
        slope = half + 0.5 * upper * (1.0 - tanh * tanh) * (const * (1.0 + 3.0 * 0.044715 * square))
        grad_upper = (nt(seed, w_down[cols, :]) * slope).astype(BF16)
        grad_up_low[:, cols] = grad_upper
        grad_second = grad_second + nt(grad_upper, w_up[:, cols])
    layer_out[...] = layer.astype(BF16)
    hat = norm_hat[...]
    scaled = grad_second * gain[...]
    back = scale * (
        scaled
        - jnp.mean(scaled, axis=-1, keepdims=True)
        - hat * jnp.mean(scaled * hat, axis=-1, keepdims=True)
    )
    grad_resid = (seed.astype(F32) + back).astype(BF16)
    res_rows[...] = grad_resid
    grad_att = nt(grad_resid, w_out[...])
    att_grad[...] = grad_att.astype(BF16)
    att_t = grad_att.T.astype(BF16)
    for h in range(HEADS):
        mg_part[h] = nn(att_t[h * DH : (h + 1) * DH, :], wlow[h, 0:RB, :])
    meet()
    mz_copies = [
        send(mg_part.at[lax.rem(z + k, NZ)], mg_z.at[k - 1], sem_mz, k - 1, peer_z(z, y, k))
        for k in ORDER
    ]
    for copy in mz_copies:
        copy.start()
    seed = cotangent[...]
    for j in range(FF // D):
        cols = slice(j * D, (j + 1) * D)
        down = nn(low_hidden[:, cols].astype(F32).T.astype(BF16), seed)
        big[2 * j : 2 * j + 2, :, 0:DH, :] = down.reshape(2, NY, DH, D)
        up = nn(low_up[...].astype(F32).T.astype(BF16), grad_up_low[:, cols])
        big[:, :, DH + 8 * j : DH + 8 * j + 8, :] = up.reshape(NZ, NY, 8, D)
    out = nn(att_rows[...].astype(F32).T.astype(BF16), res_rows[...])
    big[:, :, 2 * DH : BIG, :] = out.reshape(NZ, NY, 8, D)
    num_m[...] = jnp.zeros_like(num_m)
    geo_m[...] = jnp.zeros_like(geo_m)
    for copy in mz_copies:
        copy.wait_recv()
    total = mg_part[z]
    for k in range(NZ - 1):
        total = total + mg_z[k]
    mg_y[0] = total
    my_copies = [send(mg_y.at[0], mg_y.at[k], sem_my, k - 1, peer_y(z, y, k)) for k in range(1, NY)]
    for copy in my_copies:
        copy.start()
    by_copies = [
        send(big.at[:, lax.rem(y + k, NY)], big_y.at[k - 1], sem_by, k - 1, peer_y(z, y, k))
        for k in (2, 1, 3)
    ]
    for copy in by_copies:
        copy.start()
    for b in range(3):
        rows = slice(b * RB, (b + 1) * RB)
        mid_t[:, rows] = mids[rows, :].astype(F32).T.astype(BF16)
        normed_t[:, rows] = normed[rows, :].astype(F32).T.astype(BF16)
    acc_feat[...] = jnp.zeros_like(acc_feat)
    acc_mid[...] = jnp.zeros_like(acc_mid)
    slice_part[...] = jnp.zeros_like(slice_part)
    for copy in my_copies:
        copy.wait_recv()
    grad = mg_y[y]
    for other in range(1, NY):
        grad = grad + mg_y[lax.rem(y + NY - other, NY)]
    attention = attn[...]
    keys = keyval[0]
    values = keyval[1]
    query = query_in[...]
    both = both_in[...]
    d_value = nt(grad, attention, HIGH)
    d_attn = tn(values, grad, HIGH)
    inner = jnp.sum(attention * d_attn, axis=0, keepdims=True)
    d_score = attention * (d_attn - inner) * (1.0 / math.sqrt(DH))
    d_query = nn(keys, d_score, HIGH)
    d_key = nt(query, d_score, HIGH)
    d_both = nn(w_key[...], d_key, HIGH) + nn(w_value[...], d_value, HIGH)
    d_field = d_both[:, 0:M] + nn(w_query[...], d_query, HIGH)
    d_geo = d_both[:, M : 2 * M]
    den = sums_in[2 * DH : 2 * DH + 1, :] + EPS
    geo_den = sums_in[2 * DH + 1 : 2 * DH + 2, :] + EPS
    scaled_field = d_field / den
    scaled_geo = d_geo / geo_den
    gbuf[z, 0:DH, :] = scaled_field
    gbuf[z, DH : 2 * DH, :] = scaled_geo
    den_grad = -jnp.sum(scaled_field * both[:, 0:M], axis=0, keepdims=True)
    geo_den_grad = -jnp.sum(scaled_geo * both[:, M : 2 * M], axis=0, keepdims=True)
    pick = lax.broadcasted_iota(jnp.int32, (8, M), 0)
    gbuf[z, 2 * DH : SUMS, :] = jnp.where(pick == 0, den_grad, jnp.where(pick == 1, geo_den_grad, 0.0))
    g_copies = [send(gbuf.at[z], gbuf.at[z], sem_g, k - 1, peer_z(z, y, k)) for k in range(1, NZ)]
    for copy in g_copies:
        copy.start()
    mix_buf[z, :, 0:DH] = nt(both[:, 0:M], d_query, HIGH)
    mix_buf[z, :, DH : 2 * DH] = nt(both, d_key, HIGH)
    mix_buf[z, :, 2 * DH : 3 * DH] = nt(both, d_value, HIGH)
    mix_buf[z, :, 3 * DH : 4 * DH] = jnp.zeros((DH, DH), F32)
    mix_copies = [
        send(mix_buf.at[z], mix_buf.at[z], sem_mix, k - 1, peer_z(z, y, k)) for k in ORDER
    ]
    for copy in mix_copies:
        copy.start()
    live = lax.broadcasted_iota(jnp.int32, (RB, 1), 0) < counts[0]
    valid = jnp.where(live, 1.0, 0.0).astype(F32)

    def head_step(k, carry):
        h = lax.rem(z + NZ - k, NZ)

        @pl.when(k > 0)
        def _():
            send(gbuf.at[z], gbuf.at[h], sem_g, k - 1, peer_z(z, y, k)).wait_recv()

        row = pl.multiple_of(h * DH, DH)
        num_m[h, pl.ds(row, DH), :] = gbuf[h, 0:DH, :].astype(BF16)
        geo_m[h, pl.ds(row, DH), :] = gbuf[h, DH : 2 * DH, :].astype(BF16)
        factor = sharp[h]
        for b in range(3):
            rows = slice(b * RB, (b + 1) * RB)
            token = num_m[h] if b == 0 else geo_m[h]
            grad_w = nn(feats[rows, :], token)
            if b == 0:
                grad_w = grad_w + nn(att_grad[...], mixm[h])
                grad_w = (grad_w + gbuf[h, 2 * DH : 2 * DH + 1, :]) * valid
            else:
                grad_w = grad_w + gbuf[h, 2 * DH + 1 : 2 * DH + 2, :]
            share = shares[h, rows, :]
            inside = jnp.sum(share * grad_w, axis=-1, keepdims=True)
            low = (share * (grad_w - inside) * factor).astype(BF16)
            slice_part[...] += nn(mid_t[pl.ds(row, DH), rows], low).reshape(NY, 8, M)
            acc_mid[rows, :] += nt(low, wsm[h])
            acc_feat[rows, :] += nt(wlow[h, rows, :], token)
        return carry

    lax.fori_loop(0, NZ, head_step, 0)
    feat_total = nn(normed_t[...], acc_feat[...].astype(BF16))
    mid_total = nn(normed_t[...], acc_mid[...].astype(BF16))
    small[:, :, 0:8, :] = feat_total.reshape(NZ, NY, 8, D)
    small[:, :, 8:16, :] = mid_total.reshape(NZ, NY, 8, D)
    sy_copies = [
        send(small.at[:, lax.rem(y + k, NY)], small_y.at[k - 1], sem_sy, k - 1, peer_y(z, y, k))
        for k in (2, 1, 3)
    ]
    ly_copies = [
        send(slice_part.at[lax.rem(y + k, NY)], slice_y.at[k - 1], sem_ly, k - 1, peer_y(z, y, k))
        for k in (2, 1, 3)
    ]
    for copy in sy_copies + ly_copies:
        copy.start()
    for copy in by_copies:
        copy.wait_recv()
    big_stage[...] = ((big[:, y] + big_y[0]) + big_y[1]) + big_y[2]
    bz_copies = [
        send(big_stage.at[lax.rem(z + k, NZ)], big_z.at[k - 1], sem_bz, k - 1, peer_z(z, y, k))
        for k in ORDER
    ]
    for copy in bz_copies:
        copy.start()
    for copy in sy_copies + ly_copies:
        copy.wait_recv()
    small_stage[...] = ((small[:, y] + small_y[0]) + small_y[1]) + small_y[2]
    slice_z[0] = ((slice_part[y] + slice_y[0]) + slice_y[1]) + slice_y[2]
    lz_copies = [send(slice_z.at[0], slice_z.at[k], sem_lz, k - 1, peer_z(z, y, k)) for k in ORDER]
    sz_copies = [
        send(small_stage.at[lax.rem(z + k, NZ)], small_z.at[k - 1], sem_sz, k - 1, peer_z(z, y, k))
        for k in ORDER
    ]
    for copy in lz_copies + sz_copies:
        copy.start()
    for copy in mix_copies:
        copy.wait_recv()
    mix = mix_buf[0]
    for h in range(1, HEADS):
        mix = mix + mix_buf[h]
    for i in range(3):
        mix_grad[i] = mix[:, i * DH : (i + 1) * DH]
    for copy in lz_copies:
        copy.wait_recv()
    slices = slice_z[z]
    for other in range(1, NZ):
        slices = slices + slice_z[lax.rem(z + NZ - other, NZ)]
    slice_all[y] = slices
    la_copies = [
        send(slice_all.at[y], slice_all.at[y], sem_la, k - 1, peer_y(z, y, k)) for k in (2, 1, 3)
    ]
    for copy in la_copies:
        copy.start()
    for copy in bz_copies:
        copy.wait_recv()
    total = big_stage[z]
    for k in range(NZ - 1):
        total = total + big_z[k]
    down_grad[...] = total[0:DH]
    for j in range(FF // D):
        up_grad[:, j * D : (j + 1) * D] = total[DH + 8 * j : DH + 8 * j + 8]
    out_grad[...] = total[2 * DH : BIG]
    for copy in sz_copies:
        copy.wait_recv()
    total = small_stage[z]
    for k in range(NZ - 1):
        total = total + small_z[k]
    feat_grad[...] = total[0:8]
    mid_grad[...] = total[8:16]
    for copy in la_copies:
        copy.wait_recv()
    slice_grad[...] = slice_all[...].reshape(DH, M)
    for copies in (
        mz_copies,
        my_copies,
        by_copies,
        g_copies,
        mix_copies,
        sy_copies,
        ly_copies,
        bz_copies,
        lz_copies,
        sz_copies,
        la_copies,
    ):
        for copy in copies:
            copy.wait_send()


def shape(dims, kind=F32):
    return jax.ShapeDtypeStruct(dims, kind)


def on_device(
    points,
    geometry,
    counts,
    cotangent,
    gain_attn,
    w_feat,
    w_mid,
    w_slice,
    sharpness,
    w_query,
    w_key,
    w_value,
    w_out,
    gain_mlp,
    w_up,
    w_down,
):
    vmem = pl.BlockSpec(memory_space=pltpu.VMEM)
    smem = pl.BlockSpec(memory_space=pltpu.SMEM)
    rows = 3 * RB

    def sems(count):
        return pltpu.SemaphoreType.DMA((2, count))

    first = pl.pallas_call(
        first_kernel,
        out_shape=(
            shape((rows, D), BF16),
            shape((rows, D), BF16),
            shape((rows, D), BF16),
            shape((HEADS, rows, M)),
            shape((HEADS, rows, M), BF16),
            shape((HEADS, D, M), BF16),
            shape((HEADS, DH, M)),
            shape((2 * M, M)),
            shape((DH, 2 * M)),
            shape((DH, M)),
            shape((2, DH, 2 * M)),
            shape((SUMS, M)),
        ),
        in_specs=[vmem, vmem, smem, vmem, vmem, vmem, vmem, smem, vmem, vmem, vmem],
        out_specs=(vmem,) * 12,
        scratch_shapes=[
            pltpu.VMEM((HEADS, SUMS, M), F32),
            pltpu.VMEM((NZ - 1, SUMS, M), F32),
            pltpu.VMEM((NY, SUMS, M), F32),
            pltpu.VMEM((HEADS, DH, M), F32),
            pltpu.VMEM((D, rows), BF16),
            sems(NZ - 1),
            sems(NY - 1),
            sems(NZ - 1),
        ],
        compiler_params=pltpu.CompilerParams(
            collective_id=0, has_side_effects=True, vmem_limit_bytes=VMEM_BYTES
        ),
        name="slice_sums_and_mixing",
    )
    gain_row = gain_attn.reshape(1, D)
    normed, feats, mids, shares, wlow, wsm, mixed, attn, both, query, keyval, sums = first(
        points, geometry, counts, gain_row, w_feat, w_mid, w_slice, sharpness, w_query, w_key, w_value
    )
    second = pl.pallas_call(
        second_kernel,
        out_shape=(
            shape((RB, D), BF16),
            shape((8, D)),
            shape((8, D)),
            shape((8, D)),
            shape((8, FF)),
            shape((DH, D)),
            shape((DH, M)),
            shape((3, DH, DH)),
        ),
        in_specs=[vmem, vmem, smem] + [vmem] * 12 + [smem] + [vmem] * 7,
        out_specs=(vmem,) * 8,
        scratch_shapes=[
            pltpu.VMEM((HEADS, D, M), BF16),
            pltpu.VMEM((HEADS, D, M), BF16),
            pltpu.VMEM((HEADS, D, M), BF16),
            pltpu.VMEM((RB, D), BF16),
            pltpu.VMEM((RB, FF), BF16),
            pltpu.VMEM((RB, FF), BF16),
            pltpu.VMEM((RB, D), F32),
            pltpu.VMEM((RB, D), BF16),
            pltpu.VMEM((RB, D), BF16),
            pltpu.VMEM((RB, D), BF16),
            pltpu.VMEM((D, rows), BF16),
            pltpu.VMEM((D, rows), BF16),
            pltpu.VMEM((rows, D), F32),
            pltpu.VMEM((rows, D), F32),
            pltpu.VMEM((HEADS, DH, M), F32),
            pltpu.VMEM((NZ - 1, DH, M), F32),
            pltpu.VMEM((NY, DH, M), F32),
            pltpu.VMEM((HEADS, SUMS, M), F32),
            pltpu.VMEM((HEADS, DH, 4 * DH), F32),
            pltpu.VMEM((NZ, NY, BIG, D), F32),
            pltpu.VMEM((NY - 1, NZ, BIG, D), F32),
            pltpu.VMEM((NZ, BIG, D), F32),
            pltpu.VMEM((NZ - 1, BIG, D), F32),
            pltpu.VMEM((NZ, NY, SMALL, D), F32),
            pltpu.VMEM((NY - 1, NZ, SMALL, D), F32),
            pltpu.VMEM((NZ, SMALL, D), F32),
            pltpu.VMEM((NZ - 1, SMALL, D), F32),
            pltpu.VMEM((NY, 8, M), F32),
            pltpu.VMEM((NY - 1, 8, M), F32),
            pltpu.VMEM((NZ, 8, M), F32),
            pltpu.VMEM((NY, 8, M), F32),
            sems(NZ - 1),
            sems(NY - 1),
            sems(NZ - 1),
            sems(NZ - 1),
            sems(NY - 1),
            sems(NZ - 1),
            sems(NY - 1),
            sems(NZ - 1),
            sems(NY - 1),
            sems(NZ - 1),
            sems(NY - 1),
        ],
        compiler_params=pltpu.CompilerParams(
            collective_id=1, has_side_effects=True, vmem_limit_bytes=VMEM_BYTES
        ),
        name="mlp_and_backward",
    )
    return second(
        points,
        cotangent,
        counts,
        wlow,
        shares,
        normed,
        feats,
        mids,
        wsm,
        mixed,
        attn,
        both,
        query,
        keyval,
        sums,
        sharpness,
        gain_mlp.reshape(1, D),
        w_out,
        w_up,
        w_down,
        w_query,
        w_key,
        w_value,
    )


def solution(mesh):
    rows = P(("design", "pts"), None)
    return jax.shard_map(
        on_device,
        mesh=mesh,
        in_specs=(rows, rows, P(("design", "pts")), rows) + (P(),) * 12,
        out_specs=(rows,) * 6 + (P("design", None), P("design", None, None)),
        check_vma=False,
    )
```

time: 870 us -> 134 us (0.15)
  waiting for transfers between devices: 416 us -> 0 us
  blocking collectives: 287 us -> 0 us
  Pallas kernels: 9.67 us -> 122 us
  matrix products: 89.7 us -> 0 us
  other arithmetic: 27.1 us -> 0 us
  between operations: 15.8 us -> 1.3 us
    psum x2 -> x0, blocking collectives: 287 us -> none  [the longest x1 147 us: on_device(): lax.psum((field_sums[0], field_sums[1], geo_sums[0], geo_sums[1]), 'pts')]
    reduce_scatter x2 -> x0, waiting for transfers between devices: 277 us -> none  [the longest x1 217 us: on_device(): lax.psum_scatter(outer_rows(hidden, cotangent), 'pts', scatter_dimension=...]
    psum x2 -> x0, waiting for transfers between devices: 140 us -> none  [the longest x1 140 us: on_device(): mixed_grad = lax.psum(mixed_term, 'pts')]
    pallas_call x0 -> x2, Pallas kernels: none -> 122 us  [the longest x1 74.4 us: on_device(): second(points, cotangent, counts, wlow, shares, normed, feats, mids, wsm,...]
    dot_general x41 -> x0, matrix products: 73.6 us -> none  [the longest x3 13.3 us: mix_tokens(): jnp.einsum('hmf,hkf->hmk', query, key_rows, precision=highest)]
    sub x3 -> x0, matrix products: 16.1 us -> none  [the longest x1 10.2 us: point_back(): grad_weights - inner]
    sub x1 -> x0, other arithmetic: 11.1 us -> none  [point_back(): grad_weights - inner]
    reduce_sum x10 -> x0, other arithmetic: 9.89 us -> none  [the longest x2 4.7 us: step(): jnp.sum(weights, axis=0)]
  transfers between devices with their start and end apart: 4 -> 0, of which waited for: 3 -> 0; matrix products, arithmetic and copies ran while one was open for 3% -> 0% of each run, Pallas kernels for 0% -> 0%
where the time goes in v1:
time: 134 us
  Pallas kernels  122 us (91%)
  local copies, waits for them, and re-layouts  11 us (8%)
    pallas_call x1, Pallas kernels, on_device(): second(points, cotangent, counts, wlow, shares, normed, feats, mids, wsm,...  74.4 us
    pallas_call x1, Pallas kernels, on_device(): first(points, geometry, counts, gain_row, w_feat, w_mid, w_slice, sharpne...  47.3 us
    unnamed x8, local copies, waits for them, and re-layouts  11 us

profile of v1, /device:TPU:4, one launch (start us, length us, event | category | flops | bytes accessed | tf_op | source)
XLA Modules:
  0.0 134.0 jit_solution(3017396646080858833)
XLA Ops:
  1.3 47.3 %slice_sums_and_mixing.1 = (bf16[768,256]{1,0:T(8,128)(2,1)}, bf16[768,256]{1,0:T(8,128)(2,1)}, bf16[768,256]{1,0:T(8,128)(2,1)}, f32[8,768,256]{2,1,0:T(8,128)}...) custom-call(bf16[256,256]{1,0:T(8,128)(2,1)} %points.3, ...), custom_call_target="tpu_custom_call" | custom-call | tf_op jit(solution)/shard_map/slice_sums_and_mixing/pallas_call | solution.py:607
  48.6 74.4 %mlp_and_backward.1 = (bf16[256,256]{1,0:T(8,128)(2,1)}, f32[8,256]{1,0:T(8,128)}, f32[8,256]{1,0:T(8,128)}, f32[8,256]{1,0:T(8,128)}, f32[8,1024]{1,0:T(8,128)}...) custom-call(bf16[256,256]{1,0:T(8,128)(2,1)} %points.3, bf16[256,256]{1,0:T(8,128)(2,1)} %cotangent.1, ...), custom_call_target="tpu_custom_call" | custom-call | tf_op jit(solution)/shard_map/mlp_and_backward/pallas_call | solution.py:673
  123.0 1.6 %copy.33 = bf16[256,256]{1,0:T(8,128)(2,1)} copy(bf16[256,256]{1,0:T(8,128)(2,1)} %get-tuple-element.40) | data formatting | bytes 262144
  124.6 1.3 copy.34
  125.8 1.3 copy.35
  127.1 1.3 copy.36
  128.4 1.4 %copy.37 = f32[8,1024]{1,0:T(8,128)} copy(f32[8,1024]{1,0:T(8,128)} %get-tuple-element.44) | data formatting | bytes 65536
  129.8 1.4 %copy.38 = f32[32,256]{1,0:T(8,128)} copy(f32[32,256]{1,0:T(8,128)} %get-tuple-element.45) | data formatting | bytes 65536
  131.2 1.4 %copy.39 = f32[32,256]{1,0:T(8,128)} copy(f32[32,256]{1,0:T(8,128)} %get-tuple-element.46) | data formatting | bytes 65536
  132.6 1.4 %copy.40 = f32[3,32,32]{2,1,0:T(8,128)} copy(f32[3,32,32]{2,1,0:T(8,128)} %get-tuple-element.47) | data formatting | bytes 24576

commit v2 on v1

v2 whole, which is shorter than its diff:
```python
import math

import jax
import jax.numpy as jnp
from jax import lax
from jax.experimental import pallas as pl
from jax.experimental.pallas import tpu as pltpu
from jax.sharding import PartitionSpec as P

F32 = jnp.float32
BF16 = jnp.bfloat16
HIGH = lax.Precision.HIGHEST
NY = 4
NZ = 8
HEADS = 8
DH = 32
M = 256
D = 256
FF = 1024
RB = 256
SUMS = 72
BIG = 40
SMALL = 16
ROWS = 120
EPS = 1e-05
VMEM_BYTES = 64000000
ORDER = (4, 3, 5, 2, 6, 1, 7)


def nn(a, b, precision=None):
    return lax.dot_general(
        a, b, (((1,), (0,)), ((), ())), precision=precision, preferred_element_type=F32
    )


def nt(a, b, precision=None):
    return lax.dot_general(
        a, b, (((1,), (1,)), ((), ())), precision=precision, preferred_element_type=F32
    )


def tn(a, b, precision=None):
    return lax.dot_general(
        a, b, (((0,), (0,)), ((), ())), precision=precision, preferred_element_type=F32
    )


def norm_parts(x):
    centre = jnp.mean(x, axis=-1, keepdims=True)
    shifted = x - centre
    spread = jnp.mean(shifted * shifted, axis=-1, keepdims=True)
    scale = lax.rsqrt(spread + EPS)
    return shifted * scale, scale


def place():
    me = lax.axis_index("pts")
    return lax.div(me, NY), lax.rem(me, NY)


def peer_z(z, y, k):
    return {"pts": lax.rem(z + k, NZ) * NY + y}


def peer_y(z, y, k):
    return {"pts": z * NY + lax.rem(y + k, NY)}


def greet(z, y):
    barrier = pltpu.get_barrier_semaphore()
    for k in range(1, NZ):
        pl.semaphore_signal(barrier, inc=1, device_id=peer_z(z, y, k), device_id_type=pl.DeviceIdType.MESH)
    for k in range(1, NY):
        pl.semaphore_signal(barrier, inc=1, device_id=peer_y(z, y, k), device_id_type=pl.DeviceIdType.MESH)


def meet():
    pl.semaphore_wait(pltpu.get_barrier_semaphore(), NZ - 1 + NY - 1)


def send(src, dst, sems, slot, device):
    return pltpu.make_async_remote_copy(
        src_ref=src,
        dst_ref=dst,
        send_sem=sems.at[0, slot],
        recv_sem=sems.at[1, slot],
        device_id=device,
        device_id_type=pl.DeviceIdType.MESH,
    )


def swing(k):
    return 4 + (1 - 2 * lax.rem(k, 2)) * lax.div(k + 1, 2)


def layer_kernel(
    points,
    geometry,
    cotangent,
    counts,
    sharp,
    gain_attn,
    gain_mlp,
    w_feat,
    w_mid,
    w_slice,
    w_query,
    w_key,
    w_value,
    w_out,
    w_up,
    w_down,
    layer_out,
    packed,
    mix_grad,
    normed_t,
    feats,
    feat_t,
    mids,
    mid_t,
    shares,
    wlow,
    wsm,
    mixm,
    num_m,
    geo_m,
    grad_hid,
    low_up,
    grad_up_low,
    att_rows,
    res_rows,
    att_grad,
    acc_feat,
    acc_mid,
    part,
    zbuf,
    ybuf,
    mbuf,
    mg_part,
    mg_z,
    mg_y,
    gbuf,
    mix_buf,
    down,
    down_y,
    down_stage,
    down_z,
    big,
    big_y,
    big_stage,
    big_z,
    small,
    small_y,
    small_stage,
    small_z,
    slice_part,
    slice_y,
    slice_z,
    slice_all,
    sem_z,
    sem_y,
    sem_m,
    sem_mz,
    sem_my,
    sem_g,
    sem_mix,
    sem_dy,
    sem_dz,
    sem_by,
    sem_bz,
    sem_sy,
    sem_sz,
    sem_ly,
    sem_lz,
    sem_la,
):
    z, y = place()
    greet(z, y)
    wsm[...] = jnp.zeros_like(wsm)
    for h in range(HEADS):
        wsm[h, h * DH : (h + 1) * DH, :] = w_slice[...]
    for b in range(3):
        rows = slice(b * RB, (b + 1) * RB)
        x = points[...] if b == 0 else geometry[(b - 1) * RB : b * RB, :]
        normed = norm_parts(x.astype(F32))[0] * gain_attn[...]
        normed_t[:, rows] = normed.T.astype(BF16)
        normed = normed.astype(BF16)
        found = nn(normed, w_feat[...])
        feats[rows, :] = found.astype(BF16)
        feat_t[:, rows] = found.T.astype(BF16)
        mids[rows, :] = nn(normed, w_mid[...]).astype(BF16)
    live = lax.broadcasted_iota(jnp.int32, (RB, 1), 0) < counts[0]
    valid = jnp.where(live, 1.0, 0.0).astype(F32)
    pick = lax.broadcasted_iota(jnp.int32, (8, M), 0)
    meet()

    def sums_step(k, carry):
        h = lax.rem(z + swing(k), NZ)
        weight = wsm[h]
        factor = sharp[h]
        row = pl.multiple_of(h * DH, DH)
        numers = []
        denoms = []
        for b in range(3):
            rows = slice(b * RB, (b + 1) * RB)
            logits = nn(mids[rows, :], weight) * factor
            powers = jnp.exp(logits - jnp.max(logits, axis=-1, keepdims=True))
            share = powers * (1.0 / jnp.sum(powers, axis=-1, keepdims=True))
            shares[h, rows, :] = share
            weights = share * valid if b == 0 else share
            low = weights.astype(BF16)
            wlow[h, rows, :] = low
            denoms.append(jnp.sum(weights, axis=0, keepdims=True))
            numers.append(nn(feat_t[pl.ds(row, DH), rows], low))
        part[h, 0:DH, :] = numers[0]
        part[h, DH : 2 * DH, :] = numers[1] + numers[2]
        part[h, 2 * DH : SUMS, :] = jnp.where(
            pick == 0, denoms[0], jnp.where(pick == 1, denoms[1] + denoms[2], 0.0)
        )

        @pl.when(k < NZ - 1)
        def _():
            send(part.at[h], zbuf.at[k], sem_z, k, peer_z(z, y, swing(k))).start()

        return carry

    lax.fori_loop(0, NZ, sums_step, 0)
    for b in range(3):
        rows = slice(b * RB, (b + 1) * RB)
        mid_t[:, rows] = mids[rows, :].astype(F32).T.astype(BF16)
    mixm[...] = jnp.zeros_like(mixm)
    num_m[...] = jnp.zeros_like(num_m)
    geo_m[...] = jnp.zeros_like(geo_m)
    z_copies = [
        send(part.at[lax.rem(z + k, NZ)], zbuf.at[i], sem_z, i, peer_z(z, y, k))
        for i, k in enumerate(ORDER)
    ]
    total = part[z]
    for i in range(NZ - 1):
        z_copies[i].wait_recv()
        total = total + zbuf[i]
    ybuf[0] = total
    y_copies = [send(ybuf.at[0], ybuf.at[k], sem_y, k - 1, peer_y(z, y, k)) for k in (2, 1, 3)]
    for copy in y_copies:
        copy.start()
    acc_feat[...] = jnp.zeros_like(acc_feat)
    acc_mid[...] = jnp.zeros_like(acc_mid)
    slice_part[...] = jnp.zeros_like(slice_part)
    for copy in y_copies:
        copy.wait_recv()
    sums = ybuf[y]
    for other in range(1, NY):
        sums = sums + ybuf[lax.rem(y + NY - other, NY)]
    den = sums[2 * DH : 2 * DH + 1] + EPS
    geo_den = sums[2 * DH + 1 : 2 * DH + 2] + EPS
    field = sums[0:DH] / den
    both = jnp.concatenate([field, sums[DH : 2 * DH] / geo_den], axis=1)
    query = tn(w_query[...], field, HIGH)
    keys = tn(w_key[...], both, HIGH)
    values = tn(w_value[...], both, HIGH)
    scores = tn(keys, query, HIGH) * (1.0 / math.sqrt(DH))
    powers = jnp.exp(scores - jnp.max(scores, axis=0, keepdims=True))
    attention = powers * (1.0 / jnp.sum(powers, axis=0, keepdims=True))
    mbuf[z] = nn(values, attention, HIGH)
    m_copies = [send(mbuf.at[z], mbuf.at[z], sem_m, k - 1, peer_z(z, y, k)) for k in ORDER]
    for copy in m_copies:
        copy.start()
    for j in range(FF // D):
        cols = slice(j * D, (j + 1) * D)
        grad_hid[:, cols] = nt(cotangent[...], w_down[cols, :])
    for copy in m_copies:
        copy.wait_recv()
    for h in range(HEADS):
        mixm[h, h * DH : (h + 1) * DH, :] = mbuf[h].astype(BF16)
    attended = nt(wlow[0, 0:RB, :], mixm[0])
    for h in range(1, HEADS):
        attended = attended + nt(wlow[h, 0:RB, :], mixm[h])
    attended = attended.astype(BF16)
    att_rows[...] = attended
    residual = points[...].astype(F32) + nn(attended, w_out[...])
    hat, scale = norm_parts(residual)
    second_low = (hat * gain_mlp[...]).astype(BF16)
    low_up[...] = second_low
    const = math.sqrt(2.0 / math.pi)
    layer = residual
    grad_second = jnp.zeros((RB, D), F32)
    for j in range(FF // D):
        cols = slice(j * D, (j + 1) * D)
        upper = nn(second_low, w_up[:, cols])
        square = upper * upper
        tanh = jnp.tanh(const * upper * (1.0 + 0.044715 * square))
        half = 0.5 * (1.0 + tanh)
        hidden = upper * half
        down[2 * j : 2 * j + 2] = nn(hidden.T.astype(BF16), cotangent[...]).reshape(2, NY, DH, D)
        layer = layer + nn(hidden.astype(BF16), w_down[cols, :])
        slope = half + 0.5 * upper * (1.0 - tanh * tanh) * (const * (1.0 + 3.0 * 0.044715 * square))
        grad_upper = (grad_hid[:, cols] * slope).astype(BF16)
        grad_up_low[:, cols] = grad_upper
        grad_second = grad_second + nt(grad_upper, w_up[:, cols])
    dy_copies = [
        send(down.at[:, lax.rem(y + k, NY)], down_y.at[k - 1], sem_dy, k - 1, peer_y(z, y, k))
        for k in (2, 1, 3)
    ]
    for copy in dy_copies:
        copy.start()
    layer_out[...] = layer.astype(BF16)
    scaled = grad_second * gain_mlp[...]
    back = scale * (
        scaled
        - jnp.mean(scaled, axis=-1, keepdims=True)
        - hat * jnp.mean(scaled * hat, axis=-1, keepdims=True)
    )
    grad_resid = (cotangent[...].astype(F32) + back).astype(BF16)
    res_rows[...] = grad_resid
    grad_att = nt(grad_resid, w_out[...])
    att_grad[...] = grad_att.astype(BF16)
    att_t = grad_att.T.astype(BF16)
    for h in range(HEADS):
        mg_part[h] = nn(att_t[h * DH : (h + 1) * DH, :], wlow[h, 0:RB, :])
    mz_copies = [
        send(mg_part.at[lax.rem(z + k, NZ)], mg_z.at[k - 1], sem_mz, k - 1, peer_z(z, y, k))
        for k in ORDER
    ]
    for copy in mz_copies:
        copy.start()
    low_up_t = low_up[...].astype(F32).T.astype(BF16)
    for j in range(FF // D):
        up = nn(low_up_t, grad_up_low[:, j * D : (j + 1) * D])
        big[:, :, 8 * j : 8 * j + 8, :] = up.reshape(NZ, NY, 8, D)
    out = nn(att_rows[...].astype(F32).T.astype(BF16), res_rows[...])
    big[:, :, DH:BIG, :] = out.reshape(NZ, NY, 8, D)
    for copy in mz_copies:
        copy.wait_recv()
    total = mg_part[z]
    for k in range(NZ - 1):
        total = total + mg_z[k]
    mg_y[0] = total
    my_copies = [
        send(mg_y.at[0], mg_y.at[k], sem_my, k - 1, peer_y(z, y, k)) for k in (2, 1, 3)
    ]
    for copy in my_copies:
        copy.start()
    by_copies = [
        send(big.at[:, lax.rem(y + k, NY)], big_y.at[k - 1], sem_by, k - 1, peer_y(z, y, k))
        for k in (2, 1, 3)
    ]
    for copy in by_copies:
        copy.start()
    for copy in dy_copies:
        copy.wait_recv()
    down_stage[...] = ((down[:, y] + down_y[0]) + down_y[1]) + down_y[2]
    dz_copies = [
        send(down_stage.at[lax.rem(z + k, NZ)], down_z.at[k - 1], sem_dz, k - 1, peer_z(z, y, k))
        for k in ORDER
    ]
    for copy in dz_copies:
        copy.start()
    for copy in my_copies:
        copy.wait_recv()
    grad = mg_y[y]
    for other in range(1, NY):
        grad = grad + mg_y[lax.rem(y + NY - other, NY)]
    d_value = nt(grad, attention, HIGH)
    d_attn = tn(values, grad, HIGH)
    inner = jnp.sum(attention * d_attn, axis=0, keepdims=True)
    d_score = attention * (d_attn - inner) * (1.0 / math.sqrt(DH))
    d_query = nn(keys, d_score, HIGH)
    d_key = nt(query, d_score, HIGH)
    d_both = nn(w_key[...], d_key, HIGH) + nn(w_value[...], d_value, HIGH)
    d_field = (d_both[:, 0:M] + nn(w_query[...], d_query, HIGH)) / den
    d_geo = d_both[:, M : 2 * M] / geo_den
    gbuf[z, 0:DH, :] = d_field
    gbuf[z, DH : 2 * DH, :] = d_geo
    den_grad = -jnp.sum(d_field * both[:, 0:M], axis=0, keepdims=True)
    geo_den_grad = -jnp.sum(d_geo * both[:, M : 2 * M], axis=0, keepdims=True)
    gbuf[z, 2 * DH : SUMS, :] = jnp.where(pick == 0, den_grad, jnp.where(pick == 1, geo_den_grad, 0.0))
    g_copies = [
        send(gbuf.at[z], gbuf.at[z], sem_g, i, peer_z(z, y, k)) for i, k in enumerate(ORDER)
    ]
    for copy in g_copies:
        copy.start()
    mix_buf[z, :, 0:DH] = nt(field, d_query, HIGH)
    mix_buf[z, :, DH : 2 * DH] = nt(both, d_key, HIGH)
    mix_buf[z, :, 2 * DH : 3 * DH] = nt(both, d_value, HIGH)
    mix_buf[z, :, 3 * DH : 4 * DH] = jnp.zeros((DH, DH), F32)
    mix_copies = [
        send(mix_buf.at[z], mix_buf.at[z], sem_mix, k - 1, peer_z(z, y, k)) for k in ORDER
    ]
    for copy in mix_copies:
        copy.start()

    def back_step(k, carry):
        away = lax.rem(swing(lax.rem(k + NZ - 1, NZ)), NZ)
        h = lax.rem(z + NZ - away, NZ)

        @pl.when(k > 0)
        def _():
            send(gbuf.at[z], gbuf.at[h], sem_g, k - 1, peer_z(z, y, away)).wait_recv()

        row = pl.multiple_of(h * DH, DH)
        num_m[h, pl.ds(row, DH), :] = gbuf[h, 0:DH, :].astype(BF16)
        geo_m[h, pl.ds(row, DH), :] = gbuf[h, DH : 2 * DH, :].astype(BF16)
        factor = sharp[h]
        for b in range(3):
            rows = slice(b * RB, (b + 1) * RB)
            token = num_m[h] if b == 0 else geo_m[h]
            grad_w = nn(feats[rows, :], token)
            if b == 0:
                grad_w = grad_w + nn(att_grad[...], mixm[h])
                grad_w = (grad_w + gbuf[h, 2 * DH : 2 * DH + 1, :]) * valid
            else:
                grad_w = grad_w + gbuf[h, 2 * DH + 1 : 2 * DH + 2, :]
            share = shares[h, rows, :]
            inside = jnp.sum(share * grad_w, axis=-1, keepdims=True)
            low = (share * (grad_w - inside) * factor).astype(BF16)
            slice_part[...] += nn(mid_t[pl.ds(row, DH), rows], low).reshape(NY, 8, M)
            acc_mid[rows, :] += nt(low, wsm[h])
            acc_feat[rows, :] += nt(wlow[h, rows, :], token)
        return carry

    lax.fori_loop(0, NZ, back_step, 0)
    feat_total = nn(normed_t[...], acc_feat[...].astype(BF16))
    small[:, :, 0:8, :] = feat_total.reshape(NZ, NY, 8, D)
    mid_total = nn(normed_t[...], acc_mid[...].astype(BF16))
    small[:, :, 8:16, :] = mid_total.reshape(NZ, NY, 8, D)
    ly_copies = [
        send(slice_part.at[lax.rem(y + k, NY)], slice_y.at[k - 1], sem_ly, k - 1, peer_y(z, y, k))
        for k in (2, 1, 3)
    ]
    sy_copies = [
        send(small.at[:, lax.rem(y + k, NY)], small_y.at[k - 1], sem_sy, k - 1, peer_y(z, y, k))
        for k in (2, 1, 3)
    ]
    for copy in ly_copies + sy_copies:
        copy.start()
    for copy in by_copies:
        copy.wait_recv()
    big_stage[...] = ((big[:, y] + big_y[0]) + big_y[1]) + big_y[2]
    bz_copies = [
        send(big_stage.at[lax.rem(z + k, NZ)], big_z.at[k - 1], sem_bz, k - 1, peer_z(z, y, k))
        for k in ORDER
    ]
    for copy in ly_copies:
        copy.wait_recv()
    slice_z[0] = ((slice_part[y] + slice_y[0]) + slice_y[1]) + slice_y[2]
    lz_copies = [send(slice_z.at[0], slice_z.at[k], sem_lz, k - 1, peer_z(z, y, k)) for k in ORDER]
    for copy in lz_copies + bz_copies:
        copy.start()
    for copy in dz_copies:
        copy.wait_recv()
    total = down_stage[z]
    for k in range(NZ - 1):
        total = total + down_z[k]
    packed[0:DH] = total
    for copy in mix_copies:
        copy.wait_recv()
    mix = mix_buf[0]
    for h in range(1, HEADS):
        mix = mix + mix_buf[h]
    for i in range(3):
        mix_grad[i] = mix[:, i * DH : (i + 1) * DH]
    for copy in sy_copies:
        copy.wait_recv()
    small_stage[...] = ((small[:, y] + small_y[0]) + small_y[1]) + small_y[2]
    sz_copies = [
        send(small_stage.at[lax.rem(z + k, NZ)], small_z.at[k - 1], sem_sz, k - 1, peer_z(z, y, k))
        for k in ORDER
    ]
    for copy in sz_copies:
        copy.start()
    for copy in lz_copies:
        copy.wait_recv()
    slices = slice_z[z]
    for other in range(1, NZ):
        slices = slices + slice_z[lax.rem(z + NZ - other, NZ)]
    slice_all[y] = slices
    la_copies = [
        send(slice_all.at[y], slice_all.at[y], sem_la, k - 1, peer_y(z, y, k)) for k in (2, 1, 3)
    ]
    for copy in la_copies:
        copy.start()
    for copy in bz_copies:
        copy.wait_recv()
    total = big_stage[z]
    for k in range(NZ - 1):
        total = total + big_z[k]
    packed[DH : DH + BIG] = total
    for copy in la_copies:
        copy.wait_recv()
    packed[DH + BIG + SMALL : ROWS] = slice_all[...].reshape(DH, M)
    for copy in sz_copies:
        copy.wait_recv()
    total = small_stage[z]
    for k in range(NZ - 1):
        total = total + small_z[k]
    packed[DH + BIG : DH + BIG + SMALL] = total
    for copies in (
        z_copies,
        y_copies,
        m_copies,
        dy_copies,
        dz_copies,
        mz_copies,
        my_copies,
        by_copies,
        g_copies,
        mix_copies,
        sy_copies,
        ly_copies,
        bz_copies,
        lz_copies,
        sz_copies,
        la_copies,
    ):
        for copy in copies:
            copy.wait_send()


def result_kernel(
    layer_in,
    packed,
    mix_in,
    layer_out,
    feat_grad,
    mid_grad,
    out_grad,
    up_grad,
    down_grad,
    slice_grad,
    mix_grad,
):
    layer_out[...] = layer_in[...]
    down_grad[...] = packed[0:DH]
    for j in range(FF // D):
        up_grad[:, j * D : (j + 1) * D] = packed[DH + 8 * j : DH + 8 * j + 8]
    out_grad[...] = packed[2 * DH : 2 * DH + 8]
    feat_grad[...] = packed[2 * DH + 8 : 2 * DH + 16]
    mid_grad[...] = packed[2 * DH + 16 : 2 * DH + 24]
    slice_grad[...] = packed[2 * DH + 24 : ROWS]
    mix_grad[...] = mix_in[...]


def shape(dims, kind=F32):
    return jax.ShapeDtypeStruct(dims, kind)


def on_device(
    points,
    geometry,
    counts,
    cotangent,
    gain_attn,
    w_feat,
    w_mid,
    w_slice,
    sharpness,
    w_query,
    w_key,
    w_value,
    w_out,
    gain_mlp,
    w_up,
    w_down,
):
    vmem = pl.BlockSpec(memory_space=pltpu.VMEM)
    smem = pl.BlockSpec(memory_space=pltpu.SMEM)
    rows = 3 * RB

    def held(*dims):
        return pltpu.VMEM(dims, F32)

    def low(*dims):
        return pltpu.VMEM(dims, BF16)

    along_z = pltpu.SemaphoreType.DMA((2, NZ - 1))
    along_y = pltpu.SemaphoreType.DMA((2, NY - 1))
    layer, packed, mix = pl.pallas_call(
        layer_kernel,
        out_shape=(shape((RB, D), BF16), shape((ROWS, D)), shape((3, DH, DH))),
        in_specs=[vmem] * 3 + [smem] * 2 + [vmem] * 11,
        out_specs=(vmem,) * 3,
        scratch_shapes=[
            low(D, rows),
            low(rows, D),
            low(D, rows),
            low(rows, D),
            low(D, rows),
            held(HEADS, rows, M),
            low(HEADS, rows, M),
            low(HEADS, D, M),
            low(HEADS, D, M),
            low(HEADS, D, M),
            low(HEADS, D, M),
            held(RB, FF),
            low(RB, D),
            low(RB, FF),
            low(RB, D),
            low(RB, D),
            low(RB, D),
            held(rows, D),
            held(rows, D),
            held(HEADS, SUMS, M),
            held(NZ - 1, SUMS, M),
            held(NY, SUMS, M),
            held(HEADS, DH, M),
            held(HEADS, DH, M),
            held(NZ - 1, DH, M),
            held(NY, DH, M),
            held(HEADS, SUMS, M),
            held(HEADS, DH, 4 * DH),
            held(NZ, NY, DH, D),
            held(NY - 1, NZ, DH, D),
            held(NZ, DH, D),
            held(NZ - 1, DH, D),
            held(NZ, NY, BIG, D),
            held(NY - 1, NZ, BIG, D),
            held(NZ, BIG, D),
            held(NZ - 1, BIG, D),
            held(NZ, NY, SMALL, D),
            held(NY - 1, NZ, SMALL, D),
            held(NZ, SMALL, D),
            held(NZ - 1, SMALL, D),
            held(NY, 8, M),
            held(NY - 1, 8, M),
            held(NZ, 8, M),
            held(NY, 8, M),
            along_z,
            along_y,
            along_z,
            along_z,
            along_y,
            along_z,
            along_z,
            along_y,
            along_z,
            along_y,
            along_z,
            along_y,
            along_z,
            along_y,
            along_z,
            along_y,
        ],
        compiler_params=pltpu.CompilerParams(
            collective_id=0, has_side_effects=True, vmem_limit_bytes=VMEM_BYTES
        ),
        name="layer",
    )(
        points,
        geometry,
        cotangent,
        counts,
        sharpness,
        gain_attn.reshape(1, D),
        gain_mlp.reshape(1, D),
        w_feat,
        w_mid,
        w_slice,
        w_query,
        w_key,
        w_value,
        w_out,
        w_up,
        w_down,
    )
    return pl.pallas_call(
        result_kernel,
        out_shape=(
            shape((RB, D), BF16),
            shape((8, D)),
            shape((8, D)),
            shape((8, D)),
            shape((8, FF)),
            shape((DH, D)),
            shape((DH, M)),
            shape((3, DH, DH)),
        ),
        in_specs=[vmem] * 3,
        out_specs=(vmem,) * 8,
        name="results",
    )(layer, packed, mix)


def solution(mesh):
    rows = P(("design", "pts"), None)
    return jax.shard_map(
        on_device,
        mesh=mesh,
        in_specs=(rows, rows, P(("design", "pts")), rows) + (P(),) * 12,
        out_specs=(rows,) * 6 + (P("design", None), P("design", None, None)),
        check_vma=False,
    )
```

time: 134 us -> 103 us (0.77)
  Pallas kernels: 122 us -> 102 us
  local copies, waits for them, and re-layouts: 11 us -> 0 us
    pallas_call x2, Pallas kernels: 122 us -> 102 us  [the longest x1 100 us: on_device(): pl.pallas_call(layer_kernel, out_shape=(shape((RB, D), BF16), shape((ROWS...]
    unnamed x8 -> x0, local copies, waits for them, and re-layouts: 11 us -> none
where the time goes in v2:
time: 103 us
  Pallas kernels  102 us (99%)
  between operations  1.29 us (1%)
    pallas_call x1, Pallas kernels, on_device(): pl.pallas_call(layer_kernel, out_shape=(shape((RB, D), BF16), shape((ROWS...  100 us

profile of v2, /device:TPU:4, one launch (start us, length us, event | category | flops | bytes accessed | tf_op | source)
XLA Modules:
  0.0 103.0 jit_solution(6060885565553335543)
XLA Ops:
  1.3 100.0 %layer.1 = (bf16[256,256]{1,0:T(8,128)(2,1)}, f32[120,256]{1,0:T(8,128)}, f32[3,32,32]{2,1,0:T(8,128)}) custom-call(bf16[256,256]{1,0:T(8,128)(2,1)} %points.1, bf16[512,256]{1,0:T(8,128)(2,1)} %geometry.1, bf16[256,256]{1,0:T(8,128)(2,1)} %cotangent.1, s32[1]{0:T(128)S(6)} %copy.24.counts, f32[8]{0:T(128)} %sharp.1, f32[1,256]{1,0:T(1,128)} %bitcast.2, ...), custom_call_target="tpu_custom_call" | custom-call | tf_op jit(solution)/shard_map/layer/pallas_call | solution.py:577
  101.3 1.7 %results.1 = (bf16[256,256]{1,0:T(8,128)(2,1)}, f32[8,256]{1,0:T(8,128)}, f32[8,256]{1,0:T(8,128)}, f32[8,256]{1,0:T(8,128)}, f32[8,1024]{1,0:T(8,128)}, /*index...) custom-call(bf16[256,256]{1,0:T(8,128)(2,1)} %get-tuple-element.11.layer_in, ...), custom_call_target="tpu_custom_call" | custom-call | tf_op jit(solution)/shard_map/results/pallas_call | solution.py:666

commit v3 on v2

--- a/solution.py
+++ b/solution.py
@@ -22,6 +22,7 @@
 BIG = 40
 SMALL = 16
 ROWS = 120
+CUT = 40
 EPS = 1e-05
 VMEM_BYTES = 64000000
 ORDER = (4, 3, 5, 2, 6, 1, 7)
@@ -42,6 +43,26 @@
 def tn(a, b, precision=None):
     return lax.dot_general(
         a, b, (((0,), (0,)), ((), ())), precision=precision, preferred_element_type=F32
+    )
+
+
+def split(x):
+    high = x.astype(BF16)
+    return high, (x - high.astype(F32)).astype(BF16)
+
+
+def wide(product, a, b):
+    a_high, a_low = split(a)
+    b_high, b_low = split(b)
+    return product(a_high, b_high) + (product(a_low, b_high) + product(a_high, b_low))
+
+
+def wide_tn(a, b):
+    a_high, a_low = split(a)
+    b_high, b_low = split(b)
+    return tn(
+        jnp.concatenate([a_high, a_low, a_high], axis=0),
+        jnp.concatenate([b_high, b_high, b_low], axis=0),
     )
 
 
@@ -125,13 +146,20 @@
     num_m,
     geo_m,
     grad_hid,
+    low_hidden,
     low_up,
+    low_up_t,
     grad_up_low,
     att_rows,
     res_rows,
     att_grad,
+    res_hold,
     acc_feat,
     acc_mid,
+    both_in,
+    attn,
+    d_scores,
+    mg_sum,
     part,
     zbuf,
     ybuf,
@@ -192,6 +220,7 @@
     live = lax.broadcasted_iota(jnp.int32, (RB, 1), 0) < counts[0]
     valid = jnp.where(live, 1.0, 0.0).astype(F32)
     pick = lax.broadcasted_iota(jnp.int32, (8, M), 0)
+    key_query = nt(w_key[...], w_query[...], HIGH) * (1.0 / math.sqrt(DH))
     meet()
 
     def sums_step(k, carry):
@@ -243,8 +272,6 @@
     y_copies = [send(ybuf.at[0], ybuf.at[k], sem_y, k - 1, peer_y(z, y, k)) for k in (2, 1, 3)]
     for copy in y_copies:
         copy.start()
-    acc_feat[...] = jnp.zeros_like(acc_feat)
-    acc_mid[...] = jnp.zeros_like(acc_mid)
     slice_part[...] = jnp.zeros_like(slice_part)
     for copy in y_copies:
         copy.wait_recv()
@@ -255,19 +282,21 @@
     geo_den = sums[2 * DH + 1 : 2 * DH + 2] + EPS
     field = sums[0:DH] / den
     both = jnp.concatenate([field, sums[DH : 2 * DH] / geo_den], axis=1)
-    query = tn(w_query[...], field, HIGH)
-    keys = tn(w_key[...], both, HIGH)
-    values = tn(w_value[...], both, HIGH)
-    scores = tn(keys, query, HIGH) * (1.0 / math.sqrt(DH))
+    both_in[...] = both
+    query = wide(nn, key_query, field)
+    values = wide(tn, w_value[...], both)
+    scores = wide_tn(both, query)
     powers = jnp.exp(scores - jnp.max(scores, axis=0, keepdims=True))
     attention = powers * (1.0 / jnp.sum(powers, axis=0, keepdims=True))
-    mbuf[z] = nn(values, attention, HIGH)
+    attn[...] = attention
+    mbuf[z] = wide(nn, values, attention)
     m_copies = [send(mbuf.at[z], mbuf.at[z], sem_m, k - 1, peer_z(z, y, k)) for k in ORDER]
     for copy in m_copies:
         copy.start()
     for j in range(FF // D):
         cols = slice(j * D, (j + 1) * D)
         grad_hid[:, cols] = nt(cotangent[...], w_down[cols, :])
+    key_side = wide(tn, key_query, both)
     for copy in m_copies:
         copy.wait_recv()
     for h in range(HEADS):
@@ -282,7 +311,7 @@
     second_low = (hat * gain_mlp[...]).astype(BF16)
     low_up[...] = second_low
     const = math.sqrt(2.0 / math.pi)
-    layer = residual
+    res_hold[...] = residual
     grad_second = jnp.zeros((RB, D), F32)
     for j in range(FF // D):
         cols = slice(j * D, (j + 1) * D)
@@ -292,7 +321,7 @@
         half = 0.5 * (1.0 + tanh)
         hidden = upper * half
         down[2 * j : 2 * j + 2] = nn(hidden.T.astype(BF16), cotangent[...]).reshape(2, NY, DH, D)
-        layer = layer + nn(hidden.astype(BF16), w_down[cols, :])
+        low_hidden[:, cols] = hidden.astype(BF16)
         slope = half + 0.5 * upper * (1.0 - tanh * tanh) * (const * (1.0 + 3.0 * 0.044715 * square))
         grad_upper = (grad_hid[:, cols] * slope).astype(BF16)
         grad_up_low[:, cols] = grad_upper
@@ -303,7 +332,6 @@
     ]
     for copy in dy_copies:
         copy.start()
-    layer_out[...] = layer.astype(BF16)
     scaled = grad_second * gain_mlp[...]
     back = scale * (
         scaled
@@ -323,10 +351,17 @@
     ]
     for copy in mz_copies:
         copy.start()
-    low_up_t = low_up[...].astype(F32).T.astype(BF16)
-    for j in range(FF // D):
-        up = nn(low_up_t, grad_up_low[:, j * D : (j + 1) * D])
-        big[:, :, 8 * j : 8 * j + 8, :] = up.reshape(NZ, NY, 8, D)
+    low_up_t[...] = low_up[...].astype(F32).T.astype(BF16)
+
+    def grads_step(j, carry):
+        cols = pl.ds(pl.multiple_of(j * D, D), D)
+        up = nn(low_up_t[...], grad_up_low[:, cols])
+        big[:, :, pl.ds(pl.multiple_of(8 * j, 8), 8), :] = up.reshape(NZ, NY, 8, D)
+        res_hold[...] += nn(low_hidden[:, cols], w_down[cols, :])
+        return carry
+
+    lax.fori_loop(0, FF // D, grads_step, 0)
+    layer_out[...] = res_hold[...].astype(BF16)
     out = nn(att_rows[...].astype(F32).T.astype(BF16), res_rows[...])
     big[:, :, DH:BIG, :] = out.reshape(NZ, NY, 8, D)
     for copy in mz_copies:
@@ -346,6 +381,10 @@
     ]
     for copy in by_copies:
         copy.start()
+    bz_copies = [
+        send(big_stage.at[lax.rem(z + k, NZ)], big_z.at[k - 1], sem_bz, k - 1, peer_z(z, y, k))
+        for k in ORDER
+    ]
     for copy in dy_copies:
         copy.wait_recv()
     down_stage[...] = ((down[:, y] + down_y[0]) + down_y[1]) + down_y[2]
@@ -360,68 +399,101 @@
     grad = mg_y[y]
     for other in range(1, NY):
         grad = grad + mg_y[lax.rem(y + NY - other, NY)]
-    d_value = nt(grad, attention, HIGH)
-    d_attn = tn(values, grad, HIGH)
+    mg_sum[...] = grad
+    value_side = wide(nn, w_value[...], grad)
+    d_attn = wide_tn(both, value_side)
     inner = jnp.sum(attention * d_attn, axis=0, keepdims=True)
-    d_score = attention * (d_attn - inner) * (1.0 / math.sqrt(DH))
-    d_query = nn(keys, d_score, HIGH)
-    d_key = nt(query, d_score, HIGH)
-    d_both = nn(w_key[...], d_key, HIGH) + nn(w_value[...], d_value, HIGH)
-    d_field = (d_both[:, 0:M] + nn(w_query[...], d_query, HIGH)) / den
+    d_score = attention * (d_attn - inner)
+    d_scores[...] = d_score
+    d_both = wide(nt, query, d_score) + wide(nt, value_side, attention)
+    d_field = (d_both[:, 0:M] + wide(nn, key_side, d_score)) / den
     d_geo = d_both[:, M : 2 * M] / geo_den
-    gbuf[z, 0:DH, :] = d_field
-    gbuf[z, DH : 2 * DH, :] = d_geo
     den_grad = -jnp.sum(d_field * both[:, 0:M], axis=0, keepdims=True)
     geo_den_grad = -jnp.sum(d_geo * both[:, M : 2 * M], axis=0, keepdims=True)
-    gbuf[z, 2 * DH : SUMS, :] = jnp.where(pick == 0, den_grad, jnp.where(pick == 1, geo_den_grad, 0.0))
-    g_copies = [
-        send(gbuf.at[z], gbuf.at[z], sem_g, i, peer_z(z, y, k)) for i, k in enumerate(ORDER)
-    ]
-    for copy in g_copies:
-        copy.start()
-    mix_buf[z, :, 0:DH] = nt(field, d_query, HIGH)
-    mix_buf[z, :, DH : 2 * DH] = nt(both, d_key, HIGH)
-    mix_buf[z, :, 2 * DH : 3 * DH] = nt(both, d_value, HIGH)
-    mix_buf[z, :, 3 * DH : 4 * DH] = jnp.zeros((DH, DH), F32)
-    mix_copies = [
-        send(mix_buf.at[z], mix_buf.at[z], sem_mix, k - 1, peer_z(z, y, k)) for k in ORDER
-    ]
-    for copy in mix_copies:
-        copy.start()
-
+    gbuf[z, 0:DH, :] = d_field
+    gbuf[z, DH:CUT, :] = jnp.where(pick == 0, den_grad, jnp.where(pick == 1, geo_den_grad, 0.0))
+    gbuf[z, CUT:SUMS, :] = d_geo
+
+    def relay(step, way, half, origin):
+        piece = gbuf.at[origin, half * CUT : CUT + half * DH]
+        return pltpu.make_async_remote_copy(
+            src_ref=piece,
+            dst_ref=piece,
+            send_sem=sem_g.at[0, way, half, step],
+            recv_sem=sem_g.at[1, way, half, step],
+            device_id=peer_z(z, y, 1 if way == 0 else NZ - 1),
+            device_id_type=pl.DeviceIdType.MESH,
+        )
+
+    for half in range(2):
+        for way in range(2):
+            relay(0, way, half, z).start()
     def back_step(k, carry):
-        away = lax.rem(swing(lax.rem(k + NZ - 1, NZ)), NZ)
-        h = lax.rem(z + NZ - away, NZ)
-
-        @pl.when(k > 0)
+        step = lax.div(k + 1, 2)
+        from_left = lax.rem(k, 2)
+        h = lax.rem(z + NZ + (1 - 2 * from_left) * step, NZ)
+        left = lax.rem(z + NZ - step, NZ)
+        right = lax.rem(z + step, NZ)
+
+        @pl.when(jnp.logical_and(from_left == 1, k < NZ - 3))
         def _():
-            send(gbuf.at[z], gbuf.at[h], sem_g, k - 1, peer_z(z, y, away)).wait_recv()
+            for half in range(2):
+                relay(step - 1, 0, half, left).wait_recv()
+                relay(step, 0, half, left).start()
+                relay(step - 1, 1, half, right).wait_recv()
+                relay(step, 1, half, right).start()
+
+        @pl.when(k == NZ - 3)
+        def _():
+            relay(2, 0, 0, left).wait_recv()
+            relay(3, 0, 0, left).start()
+            relay(2, 1, 1, right).wait_recv()
+            relay(3, 1, 1, right).start()
+            relay(2, 0, 1, left).wait_recv()
+            relay(2, 1, 0, right).wait_recv()
+
+        @pl.when(k == NZ - 2)
+        def _():
+            for copy in by_copies:
+                copy.wait_recv()
+            big_stage[...] = ((big[:, y] + big_y[0]) + big_y[1]) + big_y[2]
+            for copy in bz_copies:
+                copy.start()
+
+        @pl.when(k == NZ - 1)
+        def _():
+            relay(3, 0, 0, left).wait_recv()
+            relay(3, 1, 1, left).wait_recv()
 
         row = pl.multiple_of(h * DH, DH)
         num_m[h, pl.ds(row, DH), :] = gbuf[h, 0:DH, :].astype(BF16)
-        geo_m[h, pl.ds(row, DH), :] = gbuf[h, DH : 2 * DH, :].astype(BF16)
+        geo_m[h, pl.ds(row, DH), :] = gbuf[h, CUT:SUMS, :].astype(BF16)
         factor = sharp[h]
+        field_token = gbuf[h, 0:DH, :].astype(BF16)
+        geo_token = gbuf[h, CUT:SUMS, :].astype(BF16)
         for b in range(3):
             rows = slice(b * RB, (b + 1) * RB)
             token = num_m[h] if b == 0 else geo_m[h]
             grad_w = nn(feats[rows, :], token)
             if b == 0:
                 grad_w = grad_w + nn(att_grad[...], mixm[h])
-                grad_w = (grad_w + gbuf[h, 2 * DH : 2 * DH + 1, :]) * valid
+                grad_w = (grad_w + gbuf[h, DH : DH + 1, :]) * valid
             else:
-                grad_w = grad_w + gbuf[h, 2 * DH + 1 : 2 * DH + 2, :]
+                grad_w = grad_w + gbuf[h, DH + 1 : DH + 2, :]
             share = shares[h, rows, :]
             inside = jnp.sum(share * grad_w, axis=-1, keepdims=True)
             low = (share * (grad_w - inside) * factor).astype(BF16)
             slice_part[...] += nn(mid_t[pl.ds(row, DH), rows], low).reshape(NY, 8, M)
-            acc_mid[rows, :] += nt(low, wsm[h])
-            acc_feat[rows, :] += nt(wlow[h, rows, :], token)
+            acc_mid[pl.ds(row, DH), rows] = nt(w_slice[...], low).astype(BF16)
+            acc_feat[pl.ds(row, DH), rows] = nt(
+                field_token if b == 0 else geo_token, wlow[h, rows, :]
+            ).astype(BF16)
         return carry
 
     lax.fori_loop(0, NZ, back_step, 0)
-    feat_total = nn(normed_t[...], acc_feat[...].astype(BF16))
+    feat_total = nt(normed_t[...], acc_feat[...])
     small[:, :, 0:8, :] = feat_total.reshape(NZ, NY, 8, D)
-    mid_total = nn(normed_t[...], acc_mid[...].astype(BF16))
+    mid_total = nt(normed_t[...], acc_mid[...])
     small[:, :, 8:16, :] = mid_total.reshape(NZ, NY, 8, D)
     ly_copies = [
         send(slice_part.at[lax.rem(y + k, NY)], slice_y.at[k - 1], sem_ly, k - 1, peer_y(z, y, k))
@@ -433,18 +505,21 @@
     ]
     for copy in ly_copies + sy_copies:
         copy.start()
-    for copy in by_copies:
-        copy.wait_recv()
-    big_stage[...] = ((big[:, y] + big_y[0]) + big_y[1]) + big_y[2]
-    bz_copies = [
-        send(big_stage.at[lax.rem(z + k, NZ)], big_z.at[k - 1], sem_bz, k - 1, peer_z(z, y, k))
-        for k in ORDER
+    both = both_in[...]
+    back_rows = wide(nn, both, d_scores[...])
+    cross = wide(nt, both[:, 0:M], back_rows)
+    mix_buf[z, :, 0:DH] = nn(cross, w_key[...], HIGH) * (1.0 / math.sqrt(DH))
+    mix_buf[z, :, DH : 2 * DH] = tn(cross, w_query[...], HIGH) * (1.0 / math.sqrt(DH))
+    mix_buf[z, :, 2 * DH : 3 * DH] = wide(nt, wide(nn, both, attn[...]), mg_sum[...])
+    mix_buf[z, :, 3 * DH : 4 * DH] = jnp.zeros((DH, DH), F32)
+    mix_copies = [
+        send(mix_buf.at[z], mix_buf.at[z], sem_mix, k - 1, peer_z(z, y, k)) for k in ORDER
     ]
     for copy in ly_copies:
         copy.wait_recv()
     slice_z[0] = ((slice_part[y] + slice_y[0]) + slice_y[1]) + slice_y[2]
     lz_copies = [send(slice_z.at[0], slice_z.at[k], sem_lz, k - 1, peer_z(z, y, k)) for k in ORDER]
-    for copy in lz_copies + bz_copies:
+    for copy in lz_copies + mix_copies:
         copy.start()
     for copy in dz_copies:
         copy.wait_recv()
@@ -452,13 +527,6 @@
     for k in range(NZ - 1):
         total = total + down_z[k]
     packed[0:DH] = total
-    for copy in mix_copies:
-        copy.wait_recv()
-    mix = mix_buf[0]
-    for h in range(1, HEADS):
-        mix = mix + mix_buf[h]
-    for i in range(3):
-        mix_grad[i] = mix[:, i * DH : (i + 1) * DH]
     for copy in sy_copies:
         copy.wait_recv()
     small_stage[...] = ((small[:, y] + small_y[0]) + small_y[1]) + small_y[2]
@@ -479,6 +547,13 @@
     ]
     for copy in la_copies:
         copy.start()
+    for copy in mix_copies:
+        copy.wait_recv()
+    mix = mix_buf[0]
+    for h in range(1, HEADS):
+        mix = mix + mix_buf[h]
+    for i in range(3):
+        mix_grad[i] = mix[:, i * DH : (i + 1) * DH]
     for copy in bz_copies:
         copy.wait_recv()
     total = big_stage[z]
@@ -503,7 +578,6 @@
         mz_copies,
         my_copies,
         by_copies,
-        g_copies,
         mix_copies,
         sy_copies,
         ly_copies,
@@ -514,6 +588,11 @@
     ):
         for copy in copies:
             copy.wait_send()
+    for step in range(4):
+        for way in range(2):
+            for half in range(2):
+                if step < 3 or way == half:
+                    relay(step, way, half, z).wait_send()
 
 
 def result_kernel(
@@ -592,13 +671,20 @@
             low(HEADS, D, M),
             low(HEADS, D, M),
             held(RB, FF),
+            low(RB, FF),
             low(RB, D),
+            low(D, RB),
             low(RB, FF),
             low(RB, D),
             low(RB, D),
             low(RB, D),
-            held(rows, D),
-            held(rows, D),
+            held(RB, D),
+            low(D, rows),
+            low(D, rows),
+            held(DH, 2 * M),
+            held(2 * M, M),
+            held(2 * M, M),
+            held(DH, M),
             held(HEADS, SUMS, M),
             held(NZ - 1, SUMS, M),
             held(NY, SUMS, M),
@@ -629,7 +715,7 @@
             along_z,
             along_z,
             along_y,
-            along_z,
+            pltpu.SemaphoreType.DMA((2, 2, 2, 4)),
             along_z,
             along_y,
             along_z,

time: 103 us -> 101 us (0.981)
  Pallas kernels: 102 us -> 99.5 us
    pallas_call x1, Pallas kernels: 100 us -> 97.8 us  [on_device(): pl.pallas_call(layer_kernel, out_shape=(shape((RB, D), BF16), shape((ROWS...]
where the time goes in v3:
time: 101 us
  Pallas kernels  99.5 us (99%)
  between operations  1.29 us (1%)
    pallas_call x1, Pallas kernels, on_device(): pl.pallas_call(layer_kernel, out_shape=(shape((RB, D), BF16), shape((ROWS...  97.8 us

profile of v3, /device:TPU:4, one launch (start us, length us, event | category | flops | bytes accessed | tf_op | source)
XLA Modules:
  0.0 100.8 jit_solution(14427227480728663839)
XLA Ops:
  1.3 97.8 %layer.1 = (bf16[256,256]{1,0:T(8,128)(2,1)}, f32[120,256]{1,0:T(8,128)}, f32[3,32,32]{2,1,0:T(8,128)}) custom-call(bf16[256,256]{1,0:T(8,128)(2,1)} %points.1, bf16[512,256]{1,0:T(8,128)(2,1)} %geometry.1, bf16[256,256]{1,0:T(8,128)(2,1)} %cotangent.1, s32[1]{0:T(128)S(6)} %copy.24.counts, f32[8]{0:T(128)} %sharp.1, f32[1,256]{1,0:T(1,128)} %bitcast.2, ...), custom_call_target="tpu_custom_call" | custom-call | tf_op jit(solution)/shard_map/layer/pallas_call | solution.py:656
  99.1 1.7 %results.1 = (bf16[256,256]{1,0:T(8,128)(2,1)}, f32[8,256]{1,0:T(8,128)}, f32[8,256]{1,0:T(8,128)}, f32[8,256]{1,0:T(8,128)}, f32[8,1024]{1,0:T(8,128)}, /*index...) custom-call(bf16[256,256]{1,0:T(8,128)(2,1)} %get-tuple-element.11.layer_in, ...), custom_call_target="tpu_custom_call" | custom-call | tf_op jit(solution)/shard_map/results/pallas_call | solution.py:752

commit v4 on v3

--- a/solution.py
+++ b/solution.py
@@ -99,15 +99,28 @@
     pl.semaphore_wait(pltpu.get_barrier_semaphore(), NZ - 1 + NY - 1)
 
 
-def send(src, dst, sems, slot, device):
+def send(src, dst, sems, device):
     return pltpu.make_async_remote_copy(
         src_ref=src,
         dst_ref=dst,
-        send_sem=sems.at[0, slot],
-        recv_sem=sems.at[1, slot],
+        send_sem=sems.at[0],
+        recv_sem=sems.at[1],
         device_id=device,
         device_id_type=pl.DeviceIdType.MESH,
     )
+
+
+def arrived(everything, sems):
+    send(everything, everything, sems, {"pts": 0}).wait_recv()
+
+
+def sent(everything, sems):
+    send(everything, everything, sems, {"pts": 0}).wait_send()
+
+
+def start(copies):
+    for copy in copies:
+        copy.start()
 
 
 def swing(k):
@@ -160,9 +173,12 @@
     attn,
     d_scores,
     mg_sum,
-    part,
-    zbuf,
-    ybuf,
+    part_f,
+    part_g,
+    zbuf_f,
+    zbuf_g,
+    ybuf_f,
+    ybuf_g,
     mbuf,
     mg_part,
     mg_z,
@@ -185,22 +201,25 @@
     slice_y,
     slice_z,
     slice_all,
-    sem_z,
-    sem_y,
+    sem_g,
+    sem_zf,
+    sem_zg,
+    sem_yf,
+    sem_yg,
     sem_m,
     sem_mz,
     sem_my,
-    sem_g,
-    sem_mix,
     sem_dy,
     sem_dz,
     sem_by,
     sem_bz,
-    sem_sy,
+    sem_sa,
+    sem_sb,
     sem_sz,
     sem_ly,
     sem_lz,
     sem_la,
+    sem_mix,
 ):
     z, y = place()
     greet(z, y)
@@ -223,65 +242,84 @@
     key_query = nt(w_key[...], w_query[...], HIGH) * (1.0 / math.sqrt(DH))
     meet()
 
-    def sums_step(k, carry):
+    def shares_of(h, rows):
+        logits = nn(mids[rows, :], wsm[h]) * sharp[h]
+        powers = jnp.exp(logits - jnp.max(logits, axis=-1, keepdims=True))
+        return powers * (1.0 / jnp.sum(powers, axis=-1, keepdims=True))
+
+    def field_step(k, carry):
         h = lax.rem(z + swing(k), NZ)
-        weight = wsm[h]
-        factor = sharp[h]
+        row = pl.multiple_of(h * DH, DH)
+        rows = slice(0, RB)
+        share = shares_of(h, rows)
+        shares[h, rows, :] = share
+        weights = share * valid
+        low = weights.astype(BF16)
+        wlow[h, rows, :] = low
+        part_f[h] = nn(feat_t[pl.ds(row, DH), rows], low)
+        part_g[h, DH:CUT, :] = jnp.where(pick == 0, jnp.sum(weights, axis=0, keepdims=True), 0.0)
+
+        @pl.when(k < NZ - 1)
+        def _():
+            send(part_f.at[h], zbuf_f.at[k], sem_zf, peer_z(z, y, swing(k))).start()
+
+        return carry
+
+    def geo_step(k, carry):
+        h = lax.rem(z + swing(k), NZ)
         row = pl.multiple_of(h * DH, DH)
         numers = []
         denoms = []
-        for b in range(3):
+        for b in range(1, 3):
             rows = slice(b * RB, (b + 1) * RB)
-            logits = nn(mids[rows, :], weight) * factor
-            powers = jnp.exp(logits - jnp.max(logits, axis=-1, keepdims=True))
-            share = powers * (1.0 / jnp.sum(powers, axis=-1, keepdims=True))
+            share = shares_of(h, rows)
             shares[h, rows, :] = share
-            weights = share * valid if b == 0 else share
-            low = weights.astype(BF16)
+            low = share.astype(BF16)
             wlow[h, rows, :] = low
-            denoms.append(jnp.sum(weights, axis=0, keepdims=True))
+            denoms.append(jnp.sum(share, axis=0, keepdims=True))
             numers.append(nn(feat_t[pl.ds(row, DH), rows], low))
-        part[h, 0:DH, :] = numers[0]
-        part[h, DH : 2 * DH, :] = numers[1] + numers[2]
-        part[h, 2 * DH : SUMS, :] = jnp.where(
-            pick == 0, denoms[0], jnp.where(pick == 1, denoms[1] + denoms[2], 0.0)
-        )
+        part_g[h, 0:DH, :] = numers[0] + numers[1]
+        part_g[h, DH:CUT, :] = jnp.where(pick == 1, denoms[0] + denoms[1], part_g[h, DH:CUT, :])
 
         @pl.when(k < NZ - 1)
         def _():
-            send(part.at[h], zbuf.at[k], sem_z, k, peer_z(z, y, swing(k))).start()
+            send(part_g.at[h], zbuf_g.at[k], sem_zg, peer_z(z, y, swing(k))).start()
 
         return carry
 
-    lax.fori_loop(0, NZ, sums_step, 0)
+    lax.fori_loop(0, NZ, field_step, 0)
+    lax.fori_loop(0, NZ, geo_step, 0)
+    arrived(zbuf_f, sem_zf)
+    total = part_f[z]
+    for i in range(NZ - 1):
+        total = total + zbuf_f[i]
+    ybuf_f[0] = total
+    start([send(ybuf_f.at[0], ybuf_f.at[k], sem_yf, peer_y(z, y, k)) for k in (2, 1, 3)])
     for b in range(3):
         rows = slice(b * RB, (b + 1) * RB)
         mid_t[:, rows] = mids[rows, :].astype(F32).T.astype(BF16)
     mixm[...] = jnp.zeros_like(mixm)
     num_m[...] = jnp.zeros_like(num_m)
     geo_m[...] = jnp.zeros_like(geo_m)
-    z_copies = [
-        send(part.at[lax.rem(z + k, NZ)], zbuf.at[i], sem_z, i, peer_z(z, y, k))
-        for i, k in enumerate(ORDER)
-    ]
-    total = part[z]
+    slice_part[...] = jnp.zeros_like(slice_part)
+    arrived(zbuf_g, sem_zg)
+    total = part_g[z]
     for i in range(NZ - 1):
-        z_copies[i].wait_recv()
-        total = total + zbuf[i]
-    ybuf[0] = total
-    y_copies = [send(ybuf.at[0], ybuf.at[k], sem_y, k - 1, peer_y(z, y, k)) for k in (2, 1, 3)]
-    for copy in y_copies:
-        copy.start()
-    slice_part[...] = jnp.zeros_like(slice_part)
-    for copy in y_copies:
-        copy.wait_recv()
-    sums = ybuf[y]
+        total = total + zbuf_g[i]
+    ybuf_g[0] = total
+    start([send(ybuf_g.at[0], ybuf_g.at[k], sem_yg, peer_y(z, y, k)) for k in (2, 1, 3)])
+    arrived(ybuf_f.at[1:NY], sem_yf)
+    sums = ybuf_f[y]
     for other in range(1, NY):
-        sums = sums + ybuf[lax.rem(y + NY - other, NY)]
-    den = sums[2 * DH : 2 * DH + 1] + EPS
-    geo_den = sums[2 * DH + 1 : 2 * DH + 2] + EPS
-    field = sums[0:DH] / den
-    both = jnp.concatenate([field, sums[DH : 2 * DH] / geo_den], axis=1)
+        sums = sums + ybuf_f[lax.rem(y + NY - other, NY)]
+    arrived(ybuf_g.at[1:NY], sem_yg)
+    geo_sums = ybuf_g[y]
+    for other in range(1, NY):
+        geo_sums = geo_sums + ybuf_g[lax.rem(y + NY - other, NY)]
+    den = geo_sums[DH : DH + 1] + EPS
+    geo_den = geo_sums[DH + 1 : DH + 2] + EPS
+    field = sums / den
+    both = jnp.concatenate([field, geo_sums[0:DH] / geo_den], axis=1)
     both_in[...] = both
     query = wide(nn, key_query, field)
     values = wide(tn, w_value[...], both)
@@ -290,15 +328,13 @@
     attention = powers * (1.0 / jnp.sum(powers, axis=0, keepdims=True))
     attn[...] = attention
     mbuf[z] = wide(nn, values, attention)
-    m_copies = [send(mbuf.at[z], mbuf.at[z], sem_m, k - 1, peer_z(z, y, k)) for k in ORDER]
-    for copy in m_copies:
-        copy.start()
+    m_copies = [send(mbuf.at[z], mbuf.at[z], sem_m, peer_z(z, y, k)) for k in ORDER]
+    start(m_copies)
     for j in range(FF // D):
         cols = slice(j * D, (j + 1) * D)
         grad_hid[:, cols] = nt(cotangent[...], w_down[cols, :])
     key_side = wide(tn, key_query, both)
-    for copy in m_copies:
-        copy.wait_recv()
+    arrived(mbuf.at[1:NZ], sem_m)
     for h in range(HEADS):
         mixm[h, h * DH : (h + 1) * DH, :] = mbuf[h].astype(BF16)
     attended = nt(wlow[0, 0:RB, :], mixm[0])
@@ -317,21 +353,20 @@
         cols = slice(j * D, (j + 1) * D)
         upper = nn(second_low, w_up[:, cols])
         square = upper * upper
-        tanh = jnp.tanh(const * upper * (1.0 + 0.044715 * square))
-        half = 0.5 * (1.0 + tanh)
+        half = 0.5 + 0.5 * jnp.tanh(upper * (const + (0.044715 * const) * square))
         hidden = upper * half
         down[2 * j : 2 * j + 2] = nn(hidden.T.astype(BF16), cotangent[...]).reshape(2, NY, DH, D)
         low_hidden[:, cols] = hidden.astype(BF16)
-        slope = half + 0.5 * upper * (1.0 - tanh * tanh) * (const * (1.0 + 3.0 * 0.044715 * square))
+        steep = upper * (2.0 * const + (6.0 * 0.044715 * const) * square)
+        slope = half * (1.0 + steep * (1.0 - half))
         grad_upper = (grad_hid[:, cols] * slope).astype(BF16)
         grad_up_low[:, cols] = grad_upper
         grad_second = grad_second + nt(grad_upper, w_up[:, cols])
     dy_copies = [
-        send(down.at[:, lax.rem(y + k, NY)], down_y.at[k - 1], sem_dy, k - 1, peer_y(z, y, k))
+        send(down.at[:, lax.rem(y + k, NY)], down_y.at[k - 1], sem_dy, peer_y(z, y, k))
         for k in (2, 1, 3)
     ]
-    for copy in dy_copies:
-        copy.start()
+    start(dy_copies)
     scaled = grad_second * gain_mlp[...]
     back = scale * (
         scaled
@@ -346,11 +381,10 @@
     for h in range(HEADS):
         mg_part[h] = nn(att_t[h * DH : (h + 1) * DH, :], wlow[h, 0:RB, :])
     mz_copies = [
-        send(mg_part.at[lax.rem(z + k, NZ)], mg_z.at[k - 1], sem_mz, k - 1, peer_z(z, y, k))
+        send(mg_part.at[lax.rem(z + k, NZ)], mg_z.at[k - 1], sem_mz, peer_z(z, y, k))
         for k in ORDER
     ]
-    for copy in mz_copies:
-        copy.start()
+    start(mz_copies)
     low_up_t[...] = low_up[...].astype(F32).T.astype(BF16)
 
     def grads_step(j, carry):
@@ -364,38 +398,32 @@
     layer_out[...] = res_hold[...].astype(BF16)
     out = nn(att_rows[...].astype(F32).T.astype(BF16), res_rows[...])
     big[:, :, DH:BIG, :] = out.reshape(NZ, NY, 8, D)
-    for copy in mz_copies:
-        copy.wait_recv()
+    arrived(mg_z, sem_mz)
     total = mg_part[z]
     for k in range(NZ - 1):
         total = total + mg_z[k]
     mg_y[0] = total
     my_copies = [
-        send(mg_y.at[0], mg_y.at[k], sem_my, k - 1, peer_y(z, y, k)) for k in (2, 1, 3)
-    ]
-    for copy in my_copies:
-        copy.start()
+        send(mg_y.at[0], mg_y.at[k], sem_my, peer_y(z, y, k)) for k in (2, 1, 3)
+    ]
+    start(my_copies)
     by_copies = [
-        send(big.at[:, lax.rem(y + k, NY)], big_y.at[k - 1], sem_by, k - 1, peer_y(z, y, k))
+        send(big.at[:, lax.rem(y + k, NY)], big_y.at[k - 1], sem_by, peer_y(z, y, k))
         for k in (2, 1, 3)
     ]
-    for copy in by_copies:
-        copy.start()
+    start(by_copies)
     bz_copies = [
-        send(big_stage.at[lax.rem(z + k, NZ)], big_z.at[k - 1], sem_bz, k - 1, peer_z(z, y, k))
+        send(big_stage.at[lax.rem(z + k, NZ)], big_z.at[k - 1], sem_bz, peer_z(z, y, k))
         for k in ORDER
     ]
-    for copy in dy_copies:
-        copy.wait_recv()
+    arrived(down_y, sem_dy)
     down_stage[...] = ((down[:, y] + down_y[0]) + down_y[1]) + down_y[2]
     dz_copies = [
-        send(down_stage.at[lax.rem(z + k, NZ)], down_z.at[k - 1], sem_dz, k - 1, peer_z(z, y, k))
+        send(down_stage.at[lax.rem(z + k, NZ)], down_z.at[k - 1], sem_dz, peer_z(z, y, k))
         for k in ORDER
     ]
-    for copy in dz_copies:
-        copy.start()
-    for copy in my_copies:
-        copy.wait_recv()
+    start(dz_copies)
+    arrived(mg_y.at[1:NY], sem_my)
     grad = mg_y[y]
     for other in range(1, NY):
         grad = grad + mg_y[lax.rem(y + NY - other, NY)]
@@ -452,20 +480,13 @@
             relay(2, 0, 1, left).wait_recv()
             relay(2, 1, 0, right).wait_recv()
 
-        @pl.when(k == NZ - 2)
-        def _():
-            for copy in by_copies:
-                copy.wait_recv()
-            big_stage[...] = ((big[:, y] + big_y[0]) + big_y[1]) + big_y[2]
-            for copy in bz_copies:
-                copy.start()
-
         @pl.when(k == NZ - 1)
         def _():
             relay(3, 0, 0, left).wait_recv()
             relay(3, 1, 1, left).wait_recv()
 
         row = pl.multiple_of(h * DH, DH)
+        spot = pl.multiple_of(lax.rem(h - z + NZ + 2, NZ) * DH, DH)
         num_m[h, pl.ds(row, DH), :] = gbuf[h, 0:DH, :].astype(BF16)
         geo_m[h, pl.ds(row, DH), :] = gbuf[h, CUT:SUMS, :].astype(BF16)
         factor = sharp[h]
@@ -484,27 +505,42 @@
             inside = jnp.sum(share * grad_w, axis=-1, keepdims=True)
             low = (share * (grad_w - inside) * factor).astype(BF16)
             slice_part[...] += nn(mid_t[pl.ds(row, DH), rows], low).reshape(NY, 8, M)
-            acc_mid[pl.ds(row, DH), rows] = nt(w_slice[...], low).astype(BF16)
-            acc_feat[pl.ds(row, DH), rows] = nt(
+            acc_mid[pl.ds(spot, DH), rows] = nt(w_slice[...], low).astype(BF16)
+            acc_feat[pl.ds(spot, DH), rows] = nt(
                 field_token if b == 0 else geo_token, wlow[h, rows, :]
             ).astype(BF16)
         return carry
 
-    lax.fori_loop(0, NZ, back_step, 0)
-    feat_total = nt(normed_t[...], acc_feat[...])
-    small[:, :, 0:8, :] = feat_total.reshape(NZ, NY, 8, D)
-    mid_total = nt(normed_t[...], acc_mid[...])
-    small[:, :, 8:16, :] = mid_total.reshape(NZ, NY, 8, D)
-    ly_copies = [
-        send(slice_part.at[lax.rem(y + k, NY)], slice_y.at[k - 1], sem_ly, k - 1, peer_y(z, y, k))
-        for k in (2, 1, 3)
-    ]
-    sy_copies = [
-        send(small.at[:, lax.rem(y + k, NY)], small_y.at[k - 1], sem_sy, k - 1, peer_y(z, y, k))
-        for k in (2, 1, 3)
-    ]
-    for copy in ly_copies + sy_copies:
-        copy.start()
+    def narrow(which, rows):
+        feat_half = nt(normed_t[...], acc_feat[rows, :])
+        small[which, :, :, 0:8, :] = feat_half.reshape(NZ, NY, 8, D // 2)
+        mid_half = nt(normed_t[...], acc_mid[rows, :])
+        small[which, :, :, 8:SMALL, :] = mid_half.reshape(NZ, NY, 8, D // 2)
+        start(
+            [
+                send(
+                    small.at[which, :, lax.rem(y + k, NY)],
+                    small_y.at[which, k - 1],
+                    sem_sa if which == 0 else sem_sb,
+                    peer_y(z, y, k),
+                )
+                for k in (2, 1, 3)
+            ]
+        )
+
+    lax.fori_loop(0, HEADS // 2, back_step, 0)
+    narrow(0, slice(0, D // 2))
+    lax.fori_loop(HEADS // 2, HEADS, back_step, 0)
+    start(
+        [
+            send(slice_part.at[lax.rem(y + k, NY)], slice_y.at[k - 1], sem_ly, peer_y(z, y, k))
+            for k in (2, 1, 3)
+        ]
+    )
+    narrow(1, slice(D // 2, D))
+    arrived(big_y, sem_by)
+    big_stage[...] = ((big[:, y] + big_y[0]) + big_y[1]) + big_y[2]
+    start(bz_copies)
     both = both_in[...]
     back_rows = wide(nn, both, d_scores[...])
     cross = wide(nt, both[:, 0:M], back_rows)
@@ -513,81 +549,79 @@
     mix_buf[z, :, 2 * DH : 3 * DH] = wide(nt, wide(nn, both, attn[...]), mg_sum[...])
     mix_buf[z, :, 3 * DH : 4 * DH] = jnp.zeros((DH, DH), F32)
     mix_copies = [
-        send(mix_buf.at[z], mix_buf.at[z], sem_mix, k - 1, peer_z(z, y, k)) for k in ORDER
-    ]
-    for copy in ly_copies:
-        copy.wait_recv()
+        send(mix_buf.at[z], mix_buf.at[z], sem_mix, peer_z(z, y, k)) for k in ORDER
+    ]
+    arrived(slice_y, sem_ly)
     slice_z[0] = ((slice_part[y] + slice_y[0]) + slice_y[1]) + slice_y[2]
-    lz_copies = [send(slice_z.at[0], slice_z.at[k], sem_lz, k - 1, peer_z(z, y, k)) for k in ORDER]
-    for copy in lz_copies + mix_copies:
-        copy.start()
-    for copy in dz_copies:
-        copy.wait_recv()
+    lz_copies = [send(slice_z.at[0], slice_z.at[k], sem_lz, peer_z(z, y, k)) for k in ORDER]
+    start(lz_copies + mix_copies)
+    arrived(down_z, sem_dz)
     total = down_stage[z]
     for k in range(NZ - 1):
         total = total + down_z[k]
     packed[0:DH] = total
-    for copy in sy_copies:
-        copy.wait_recv()
-    small_stage[...] = ((small[:, y] + small_y[0]) + small_y[1]) + small_y[2]
+    halves = []
+    for which in range(2):
+        arrived(small_y.at[which], sem_sa if which == 0 else sem_sb)
+        halves.append(
+            ((small[which, :, y] + small_y[which, 0]) + small_y[which, 1]) + small_y[which, 2]
+        )
+    turned = jnp.concatenate(halves, axis=2).reshape(NZ * SMALL, D)
+    turned = pltpu.roll(turned, lax.rem(z + NZ - 2, NZ) * DH, 1)
+    small_stage[...] = turned.reshape(NZ, SMALL, D)
     sz_copies = [
-        send(small_stage.at[lax.rem(z + k, NZ)], small_z.at[k - 1], sem_sz, k - 1, peer_z(z, y, k))
+        send(small_stage.at[lax.rem(z + k, NZ)], small_z.at[k - 1], sem_sz, peer_z(z, y, k))
         for k in ORDER
     ]
-    for copy in sz_copies:
-        copy.start()
-    for copy in lz_copies:
-        copy.wait_recv()
+    start(sz_copies)
+    arrived(slice_z.at[1:NZ], sem_lz)
     slices = slice_z[z]
     for other in range(1, NZ):
         slices = slices + slice_z[lax.rem(z + NZ - other, NZ)]
     slice_all[y] = slices
     la_copies = [
-        send(slice_all.at[y], slice_all.at[y], sem_la, k - 1, peer_y(z, y, k)) for k in (2, 1, 3)
-    ]
-    for copy in la_copies:
-        copy.start()
-    for copy in mix_copies:
-        copy.wait_recv()
+        send(slice_all.at[y], slice_all.at[y], sem_la, peer_y(z, y, k)) for k in (2, 1, 3)
+    ]
+    start(la_copies)
+    arrived(mix_buf.at[1:NZ], sem_mix)
     mix = mix_buf[0]
     for h in range(1, HEADS):
         mix = mix + mix_buf[h]
     for i in range(3):
         mix_grad[i] = mix[:, i * DH : (i + 1) * DH]
-    for copy in bz_copies:
-        copy.wait_recv()
+    arrived(big_z, sem_bz)
     total = big_stage[z]
     for k in range(NZ - 1):
         total = total + big_z[k]
     packed[DH : DH + BIG] = total
-    for copy in la_copies:
-        copy.wait_recv()
+    arrived(slice_all.at[1:NY], sem_la)
     packed[DH + BIG + SMALL : ROWS] = slice_all[...].reshape(DH, M)
-    for copy in sz_copies:
-        copy.wait_recv()
+    arrived(small_z, sem_sz)
     total = small_stage[z]
     for k in range(NZ - 1):
         total = total + small_z[k]
     packed[DH + BIG : DH + BIG + SMALL] = total
-    for copies in (
-        z_copies,
-        y_copies,
-        m_copies,
-        dy_copies,
-        dz_copies,
-        mz_copies,
-        my_copies,
-        by_copies,
-        mix_copies,
-        sy_copies,
-        ly_copies,
-        bz_copies,
-        lz_copies,
-        sz_copies,
-        la_copies,
+    for everything, sems in (
+        (zbuf_f, sem_zf),
+        (zbuf_g, sem_zg),
+        (ybuf_f.at[1:NY], sem_yf),
+        (ybuf_g.at[1:NY], sem_yg),
+        (mbuf.at[1:NZ], sem_m),
+        (mg_z, sem_mz),
+        (mg_y.at[1:NY], sem_my),
+        (down_y, sem_dy),
+        (down_z, sem_dz),
+        (big_y, sem_by),
+        (big_z, sem_bz),
+        (small_y.at[0], sem_sa),
+        (small_y.at[1], sem_sb),
+        (small_z, sem_sz),
+        (slice_y, sem_ly),
+        (slice_z.at[1:NZ], sem_lz),
+        (slice_all.at[1:NY], sem_la),
+        (mix_buf.at[1:NZ], sem_mix),
     ):
-        for copy in copies:
-            copy.wait_send()
+        sent(everything, sems)
     for step in range(4):
         for way in range(2):
             for half in range(2):
@@ -651,8 +685,6 @@
     def low(*dims):
         return pltpu.VMEM(dims, BF16)
 
-    along_z = pltpu.SemaphoreType.DMA((2, NZ - 1))
-    along_y = pltpu.SemaphoreType.DMA((2, NY - 1))
     layer, packed, mix = pl.pallas_call(
         layer_kernel,
         out_shape=(shape((RB, D), BF16), shape((ROWS, D)), shape((3, DH, DH))),
@@ -685,9 +717,12 @@
             held(2 * M, M),
             held(2 * M, M),
             held(DH, M),
-            held(HEADS, SUMS, M),
-            held(NZ - 1, SUMS, M),
-            held(NY, SUMS, M),
+            held(HEADS, DH, M),
+            held(HEADS, CUT, M),
+            held(NZ - 1, DH, M),
+            held(NZ - 1, CUT, M),
+            held(NY, DH, M),
+            held(NY, CUT, M),
             held(HEADS, DH, M),
             held(HEADS, DH, M),
             held(NZ - 1, DH, M),
@@ -702,31 +737,17 @@
             held(NY - 1, NZ, BIG, D),
             held(NZ, BIG, D),
             held(NZ - 1, BIG, D),
-            held(NZ, NY, SMALL, D),
-            held(NY - 1, NZ, SMALL, D),
+            held(2, NZ, NY, SMALL, D // 2),
+            held(2, NY - 1, NZ, SMALL, D // 2),
             held(NZ, SMALL, D),
             held(NZ - 1, SMALL, D),
             held(NY, 8, M),
             held(NY - 1, 8, M),
             held(NZ, 8, M),
             held(NY, 8, M),
-            along_z,
-            along_y,
-            along_z,
-            along_z,
-            along_y,
             pltpu.SemaphoreType.DMA((2, 2, 2, 4)),
-            along_z,
-            along_y,
-            along_z,
-            along_y,
-            along_z,
-            along_y,
-            along_z,
-            along_y,
-            along_z,
-            along_y,
-        ],
+        ]
+        + [pltpu.SemaphoreType.DMA((2,))] * 18,
         compiler_params=pltpu.CompilerParams(
             collective_id=0, has_side_effects=True, vmem_limit_bytes=VMEM_BYTES
         ),

time: 101 us -> 95.9 us (0.950)
  Pallas kernels: 99.5 us -> 94.5 us
    pallas_call x1, Pallas kernels: 97.8 us -> 92.8 us  [on_device(): pl.pallas_call(layer_kernel, out_shape=(shape((RB, D), BF16), shape((ROWS...]
where the time goes in v4:
time: 95.9 us; the launch traced here: 95.8 us
  Pallas kernels  94.5 us (99%)
  between operations  1.29 us (1%)
    pallas_call x1, Pallas kernels, on_device(): pl.pallas_call(layer_kernel, out_shape=(shape((RB, D), BF16), shape((ROWS...  92.8 us

profile of v4, /device:TPU:4, one launch (start us, length us, event | category | flops | bytes accessed | tf_op | source)
XLA Modules:
  0.0 95.8 jit_solution(9710911871256432448)
XLA Ops:
  1.3 92.8 %layer.1 = (bf16[256,256]{1,0:T(8,128)(2,1)}, f32[120,256]{1,0:T(8,128)}, f32[3,32,32]{2,1,0:T(8,128)}) custom-call(bf16[256,256]{1,0:T(8,128)(2,1)} %points.1, bf16[512,256]{1,0:T(8,128)(2,1)} %geometry.1, bf16[256,256]{1,0:T(8,128)(2,1)} %cotangent.1, s32[1]{0:T(128)S(6)} %copy.24.counts, f32[8]{0:T(128)} %sharp.1, f32[1,256]{1,0:T(1,128)} %bitcast.2, ...), custom_call_target="tpu_custom_call" | custom-call | tf_op jit(solution)/shard_map/layer/pallas_call | solution.py:688
  94.1 1.7 %results.1 = (bf16[256,256]{1,0:T(8,128)(2,1)}, f32[8,256]{1,0:T(8,128)}, f32[8,256]{1,0:T(8,128)}, f32[8,256]{1,0:T(8,128)}, f32[8,1024]{1,0:T(8,128)}, /*index...) custom-call(bf16[256,256]{1,0:T(8,128)(2,1)} %get-tuple-element.11.layer_in, ...), custom_call_target="tpu_custom_call" | custom-call | tf_op jit(solution)/shard_map/results/pallas_call | solution.py:773

commit v5 on v4

--- a/solution.py
+++ b/solution.py
@@ -19,10 +19,12 @@
 FF = 1024
 RB = 256
 SUMS = 72
-BIG = 40
+BIG = 24
+EARLY = 24
 SMALL = 16
 ROWS = 120
 CUT = 40
+STRIP = 128
 EPS = 1e-05
 VMEM_BYTES = 64000000
 ORDER = (4, 3, 5, 2, 6, 1, 7)
@@ -184,7 +186,7 @@
     mg_z,
     mg_y,
     gbuf,
-    mix_buf,
+    mix_part,
     down,
     down_y,
     down_stage,
@@ -202,6 +204,8 @@
     slice_z,
     slice_all,
     sem_g,
+    sem_by,
+    sem_bz,
     sem_zf,
     sem_zg,
     sem_yf,
@@ -211,15 +215,12 @@
     sem_my,
     sem_dy,
     sem_dz,
-    sem_by,
-    sem_bz,
     sem_sa,
     sem_sb,
     sem_sz,
     sem_ly,
     sem_lz,
     sem_la,
-    sem_mix,
 ):
     z, y = place()
     greet(z, y)
@@ -351,22 +352,32 @@
     grad_second = jnp.zeros((RB, D), F32)
     for j in range(FF // D):
         cols = slice(j * D, (j + 1) * D)
-        upper = nn(second_low, w_up[:, cols])
-        square = upper * upper
-        half = 0.5 + 0.5 * jnp.tanh(upper * (const + (0.044715 * const) * square))
-        hidden = upper * half
-        down[2 * j : 2 * j + 2] = nn(hidden.T.astype(BF16), cotangent[...]).reshape(2, NY, DH, D)
-        low_hidden[:, cols] = hidden.astype(BF16)
-        steep = upper * (2.0 * const + (6.0 * 0.044715 * const) * square)
-        slope = half * (1.0 + steep * (1.0 - half))
-        grad_upper = (grad_hid[:, cols] * slope).astype(BF16)
-        grad_up_low[:, cols] = grad_upper
-        grad_second = grad_second + nt(grad_upper, w_up[:, cols])
-    dy_copies = [
-        send(down.at[:, lax.rem(y + k, NY)], down_y.at[k - 1], sem_dy, peer_y(z, y, k))
-        for k in (2, 1, 3)
-    ]
-    start(dy_copies)
+        for r in range(RB // STRIP):
+            strip = slice(r * STRIP, (r + 1) * STRIP)
+            upper = nn(low_up[strip, :], w_up[:, cols])
+            square = upper * upper
+            half = 0.5 + 0.5 * jnp.tanh(upper * (const + (0.044715 * const) * square))
+            hidden = upper * half
+            low_hidden[strip, cols] = hidden.astype(BF16)
+            steep = upper * (2.0 * const + (6.0 * 0.044715 * const) * square)
+            slope = half * (1.0 + steep * (1.0 - half))
+            grad_up_low[strip, cols] = (grad_hid[strip, cols] * slope).astype(BF16)
+        hidden_t = low_hidden[:, cols].T
+        found = nn(hidden_t, cotangent[...]).reshape(2, NY, DH, D)
+        down[2 * j : 2 * j + 2] = found[:, :, 0:EARLY]
+        big[1, 2 * j : 2 * j + 2, :, 16:24, :] = found[:, :, EARLY:DH]
+        start(
+            [
+                send(
+                    down.at[2 * j : 2 * j + 2, lax.rem(y + k, NY)],
+                    down_y.at[k - 1, 2 * j : 2 * j + 2],
+                    sem_dy,
+                    peer_y(z, y, k),
+                )
+                for k in (2, 1, 3)
+            ]
+        )
+        grad_second = grad_second + nt(grad_up_low[:, cols], w_up[:, cols])
     scaled = grad_second * gain_mlp[...]
     back = scale * (
         scaled
@@ -390,14 +401,17 @@
     def grads_step(j, carry):
         cols = pl.ds(pl.multiple_of(j * D, D), D)
         up = nn(low_up_t[...], grad_up_low[:, cols])
-        big[:, :, pl.ds(pl.multiple_of(8 * j, 8), 8), :] = up.reshape(NZ, NY, 8, D)
+        group = lax.div(j, 3)
+        big[group, :, :, pl.ds(pl.multiple_of(8 * (j - 3 * group), 8), 8), :] = up.reshape(
+            NZ, NY, 8, D
+        )
         res_hold[...] += nn(low_hidden[:, cols], w_down[cols, :])
         return carry
 
     lax.fori_loop(0, FF // D, grads_step, 0)
     layer_out[...] = res_hold[...].astype(BF16)
     out = nn(att_rows[...].astype(F32).T.astype(BF16), res_rows[...])
-    big[:, :, DH:BIG, :] = out.reshape(NZ, NY, 8, D)
+    big[1, :, :, 8:16, :] = out.reshape(NZ, NY, 8, D)
     arrived(mg_z, sem_mz)
     total = mg_part[z]
     for k in range(NZ - 1):
@@ -407,15 +421,36 @@
         send(mg_y.at[0], mg_y.at[k], sem_my, peer_y(z, y, k)) for k in (2, 1, 3)
     ]
     start(my_copies)
-    by_copies = [
-        send(big.at[:, lax.rem(y + k, NY)], big_y.at[k - 1], sem_by, peer_y(z, y, k))
-        for k in (2, 1, 3)
-    ]
-    start(by_copies)
-    bz_copies = [
-        send(big_stage.at[lax.rem(z + k, NZ)], big_z.at[k - 1], sem_bz, peer_z(z, y, k))
-        for k in ORDER
-    ]
+    for group in range(2):
+        start(
+            [
+                send(
+                    big.at[group, :, lax.rem(y + k, NY)],
+                    big_y.at[group, k - 1],
+                    sem_by.at[group],
+                    peer_y(z, y, k),
+                )
+                for k in (2, 1, 3)
+            ]
+        )
+
+    def spread_big(group):
+        arrived(big_y.at[group], sem_by.at[group])
+        big_stage[group] = (
+            (big[group, :, y] + big_y[group, 0]) + big_y[group, 1]
+        ) + big_y[group, 2]
+        start(
+            [
+                send(
+                    big_stage.at[group, lax.rem(z + k, NZ)],
+                    big_z.at[group, k - 1],
+                    sem_bz.at[group],
+                    peer_z(z, y, k),
+                )
+                for k in ORDER
+            ]
+        )
+
     arrived(down_y, sem_dy)
     down_stage[...] = ((down[:, y] + down_y[0]) + down_y[1]) + down_y[2]
     dz_copies = [
@@ -480,6 +515,10 @@
             relay(2, 0, 1, left).wait_recv()
             relay(2, 1, 0, right).wait_recv()
 
+        @pl.when(k == NZ - 2)
+        def _():
+            spread_big(0)
+
         @pl.when(k == NZ - 1)
         def _():
             relay(3, 0, 0, left).wait_recv()
@@ -538,28 +577,21 @@
         ]
     )
     narrow(1, slice(D // 2, D))
-    arrived(big_y, sem_by)
-    big_stage[...] = ((big[:, y] + big_y[0]) + big_y[1]) + big_y[2]
-    start(bz_copies)
     both = both_in[...]
     back_rows = wide(nn, both, d_scores[...])
     cross = wide(nt, both[:, 0:M], back_rows)
-    mix_buf[z, :, 0:DH] = nn(cross, w_key[...], HIGH) * (1.0 / math.sqrt(DH))
-    mix_buf[z, :, DH : 2 * DH] = tn(cross, w_query[...], HIGH) * (1.0 / math.sqrt(DH))
-    mix_buf[z, :, 2 * DH : 3 * DH] = wide(nt, wide(nn, both, attn[...]), mg_sum[...])
-    mix_buf[z, :, 3 * DH : 4 * DH] = jnp.zeros((DH, DH), F32)
-    mix_copies = [
-        send(mix_buf.at[z], mix_buf.at[z], sem_mix, peer_z(z, y, k)) for k in ORDER
-    ]
+    mix_part[:, 0:DH] = nn(cross, w_key[...], HIGH) * (1.0 / math.sqrt(DH))
+    mix_part[:, DH : 2 * DH] = tn(cross, w_query[...], HIGH) * (1.0 / math.sqrt(DH))
+    mix_part[:, 2 * DH : 3 * DH] = wide(nt, wide(nn, both, attn[...]), mg_sum[...])
+    mix_part[:, 3 * DH : 4 * DH] = jnp.zeros((DH, DH), F32)
     arrived(slice_y, sem_ly)
-    slice_z[0] = ((slice_part[y] + slice_y[0]) + slice_y[1]) + slice_y[2]
+    slice_z[0, 0:8, :] = ((slice_part[y] + slice_y[0]) + slice_y[1]) + slice_y[2]
+    quarter = mix_part[pl.ds(pl.multiple_of(8 * y, 8), 8), :]
+    slice_z[0, 8:16, 0 : 4 * DH] = quarter
+    slice_z[0, 8:16, 4 * DH : M] = jnp.zeros((8, M - 4 * DH), F32)
     lz_copies = [send(slice_z.at[0], slice_z.at[k], sem_lz, peer_z(z, y, k)) for k in ORDER]
-    start(lz_copies + mix_copies)
-    arrived(down_z, sem_dz)
-    total = down_stage[z]
-    for k in range(NZ - 1):
-        total = total + down_z[k]
-    packed[0:DH] = total
+    start(lz_copies)
+    spread_big(1)
     halves = []
     for which in range(2):
         arrived(small_y.at[which], sem_sa if which == 0 else sem_sb)
@@ -574,6 +606,11 @@
         for k in ORDER
     ]
     start(sz_copies)
+    arrived(down_z, sem_dz)
+    total = down_stage[z]
+    for k in range(NZ - 1):
+        total = total + down_z[k]
+    packed[0:EARLY] = total
     arrived(slice_z.at[1:NZ], sem_lz)
     slices = slice_z[z]
     for other in range(1, NZ):
@@ -583,24 +620,26 @@
         send(slice_all.at[y], slice_all.at[y], sem_la, peer_y(z, y, k)) for k in (2, 1, 3)
     ]
     start(la_copies)
-    arrived(mix_buf.at[1:NZ], sem_mix)
-    mix = mix_buf[0]
-    for h in range(1, HEADS):
-        mix = mix + mix_buf[h]
+    for group in range(2):
+        arrived(big_z.at[group], sem_bz.at[group])
+        total = big_stage[group, z]
+        for k in range(NZ - 1):
+            total = total + big_z[group, k]
+        if group == 0:
+            packed[DH : DH + 24] = total
+        else:
+            packed[DH + 24 : DH + 40] = total[0:16]
+            packed[EARLY:DH] = total[16:24]
+    arrived(slice_all.at[1:NY], sem_la)
+    packed[2 * DH + 24 : ROWS] = slice_all[:, 0:8, :].reshape(DH, M)
+    mix = slice_all[:, 8:16, 0 : 4 * DH].reshape(DH, 4 * DH)
     for i in range(3):
         mix_grad[i] = mix[:, i * DH : (i + 1) * DH]
-    arrived(big_z, sem_bz)
-    total = big_stage[z]
-    for k in range(NZ - 1):
-        total = total + big_z[k]
-    packed[DH : DH + BIG] = total
-    arrived(slice_all.at[1:NY], sem_la)
-    packed[DH + BIG + SMALL : ROWS] = slice_all[...].reshape(DH, M)
     arrived(small_z, sem_sz)
     total = small_stage[z]
     for k in range(NZ - 1):
         total = total + small_z[k]
-    packed[DH + BIG : DH + BIG + SMALL] = total
+    packed[2 * DH + 8 : 2 * DH + 24] = total
     for everything, sems in (
         (zbuf_f, sem_zf),
         (zbuf_g, sem_zg),
@@ -611,15 +650,16 @@
         (mg_y.at[1:NY], sem_my),
         (down_y, sem_dy),
         (down_z, sem_dz),
-        (big_y, sem_by),
-        (big_z, sem_bz),
+        (big_y.at[0], sem_by.at[0]),
+        (big_y.at[1], sem_by.at[1]),
+        (big_z.at[0], sem_bz.at[0]),
+        (big_z.at[1], sem_bz.at[1]),
         (small_y.at[0], sem_sa),
         (small_y.at[1], sem_sb),
         (small_z, sem_sz),
         (slice_y, sem_ly),
         (slice_z.at[1:NZ], sem_lz),
         (slice_all.at[1:NY], sem_la),
-        (mix_buf.at[1:NZ], sem_mix),
     ):
         sent(everything, sems)
     for step in range(4):
@@ -728,26 +768,27 @@
             held(NZ - 1, DH, M),
             held(NY, DH, M),
             held(HEADS, SUMS, M),
-            held(HEADS, DH, 4 * DH),
-            held(NZ, NY, DH, D),
-            held(NY - 1, NZ, DH, D),
-            held(NZ, DH, D),
-            held(NZ - 1, DH, D),
-            held(NZ, NY, BIG, D),
-            held(NY - 1, NZ, BIG, D),
-            held(NZ, BIG, D),
-            held(NZ - 1, BIG, D),
+            held(DH, 4 * DH),
+            held(NZ, NY, EARLY, D),
+            held(NY - 1, NZ, EARLY, D),
+            held(NZ, EARLY, D),
+            held(NZ - 1, EARLY, D),
+            held(2, NZ, NY, BIG, D),
+            held(2, NY - 1, NZ, BIG, D),
+            held(2, NZ, BIG, D),
+            held(2, NZ - 1, BIG, D),
             held(2, NZ, NY, SMALL, D // 2),
             held(2, NY - 1, NZ, SMALL, D // 2),
             held(NZ, SMALL, D),
             held(NZ - 1, SMALL, D),
             held(NY, 8, M),
             held(NY - 1, 8, M),
-            held(NZ, 8, M),
-            held(NY, 8, M),
+            held(NZ, 16, M),
+            held(NY, 16, M),
             pltpu.SemaphoreType.DMA((2, 2, 2, 4)),
         ]
-        + [pltpu.SemaphoreType.DMA((2,))] * 18,
+        + [pltpu.SemaphoreType.DMA((2, 2))] * 2
+        + [pltpu.SemaphoreType.DMA((2,))] * 15,
         compiler_params=pltpu.CompilerParams(
             collective_id=0, has_side_effects=True, vmem_limit_bytes=VMEM_BYTES
         ),

time: 95.9 us -> 90.7 us (0.946)
  Pallas kernels: 94.5 us -> 88.9 us
    pallas_call x1, Pallas kernels: 92.8 us -> 87.2 us  [on_device(): pl.pallas_call(layer_kernel, out_shape=(shape((RB, D), BF16), shape((ROWS...]
where the time goes in v5:
time: 90.7 us; the launch traced here: 90.2 us
  Pallas kernels  88.9 us (98%)
  between operations  1.29 us (1%)
    pallas_call x1, Pallas kernels, on_device(): pl.pallas_call(layer_kernel, out_shape=(shape((RB, D), BF16), shape((ROWS...  87.2 us

profile of v5, /device:TPU:4, one launch (start us, length us, event | category | flops | bytes accessed | tf_op | source)
XLA Modules:
  0.0 90.2 jit_solution(15906745043112324657)
XLA Ops:
  1.3 87.2 %layer.1 = (bf16[256,256]{1,0:T(8,128)(2,1)}, f32[120,256]{1,0:T(8,128)}, f32[3,32,32]{2,1,0:T(8,128)}) custom-call(bf16[256,256]{1,0:T(8,128)(2,1)} %points.1, bf16[512,256]{1,0:T(8,128)(2,1)} %geometry.1, bf16[256,256]{1,0:T(8,128)(2,1)} %cotangent.1, s32[1]{0:T(128)S(6)} %copy.24.counts, f32[8]{0:T(128)} %sharp.1, f32[1,256]{1,0:T(1,128)} %bitcast.2, ...), custom_call_target="tpu_custom_call" | custom-call | tf_op jit(solution)/shard_map/layer/pallas_call | solution.py:728
  88.5 1.7 %results.1 = (bf16[256,256]{1,0:T(8,128)(2,1)}, f32[8,256]{1,0:T(8,128)}, f32[8,256]{1,0:T(8,128)}, f32[8,256]{1,0:T(8,128)}, f32[8,1024]{1,0:T(8,128)}, /*index...) custom-call(bf16[256,256]{1,0:T(8,128)(2,1)} %get-tuple-element.11.layer_in, ...), custom_call_target="tpu_custom_call" | custom-call | tf_op jit(solution)/shard_map/results/pallas_call | solution.py:814
